TPU v7x, 512 devices: a whole 4x4x16 slice. The times are simulated.
512 devices in a mesh: row: 16 (over z), col: 16 (over x, y), layer: 2 (over core).
Axes of the slice: x: 4, y: 4, z: 16, core: 2. Of those that a mesh axis runs over, the one named last changes fastest.
Arguments:
- a_tiles: bfloat16 [16, 16, 2, 512, 512], P('row', 'col'), as said below
- a_where: int32 [16, 16, 2], P('row', 'col'), may hold values from 0 to 3, as said below
- a_count: int32 [16, 16], P('row', 'col'), may hold values from 1 to 2, as said below
- b_slab: bfloat16 [16, 16, 1024, 384], P('row', 'col'), may hold values from -6 to 6
Outputs:
- flow_next: float32 [16384, 6144], P(('row', 'layer'), 'col')
Inputs may be any that keep to these rules, and one draw needn't show every extreme that they name: `a_where`: the positions of the slots of one block are distinct. The live slots of a block are its first a_count ones; some block has all 2 slots live. `a_tiles`: entries of slots that are not live are ignored.
All inputs are finite; a program needn't handle non-finite values.
Results may differ from a plain program's by a relative error of at most 0.0003.
Values may be sent and summed in bfloat16 or wider, within the bound.
No kernel may reach another device: no remote copies, remote signals or barrier semaphores. Data moves between devices by JAX's collectives and lax.ppermute only.
A program may use at most 64 MiB of HBM per device.

v0:
```python
import jax
import jax.numpy as jnp
from jax import lax
from jax.experimental import pallas as pl
from jax.experimental.pallas import tpu as pltpu
from jax.sharding import PartitionSpec as P


SPAN = 2
SIDE = 4
PAD = 16
DEAD = SPAN * SPAN


def torus_pairs(step, layers):
    pairs = []
    for x in range(SIDE):
        for y in range(SIDE):
            for core in range(layers):
                sign = 1 - 2 * core
                to_x, to_y = (x + sign * step[0]) % SIDE, (y + sign * step[1]) % SIDE
                pairs.append(((x * SIDE + y) * layers + core, (to_x * SIDE + to_y) * layers + core))
    return pairs


def shift(value, step, sign, layers):
    return lax.ppermute(value, ("col", "layer"), torus_pairs((sign * step[0], sign * step[1]), layers))


def gather_line(value, step, layers):
    before = shift(value, step, 1, layers)
    after = shift(value, step, -1, layers)
    return [value, before, after, shift(before, step, 1, layers)]


def product_kernel(table, *refs):
    tile_refs = refs[:8]
    slab, keep, send, mass, pieces, blocks, sums, spread, order, target = refs[8:18]
    piece_sem, block_sem, out_sem = refs[18:]
    rows, depth = pieces.shape[1], blocks.shape[1]
    stride = rows + PAD

    def fetches(item, tiles, inner):
        block = table[1, item] * SPAN + table[0, item] % SPAN
        start = pl.multiple_of(block * depth, depth)
        first = pl.multiple_of(inner * stride, PAD)
        return (
            pltpu.make_async_copy(tiles.at[pl.ds(first, rows), :], pieces.at[item], piece_sem.at[item]),
            pltpu.make_async_copy(slab.at[pl.ds(start, depth), :], blocks.at[item], block_sem.at[item]),
        )

    def start(item, tiles, inner):
        for copy in fetches(item, tiles, inner):
            copy.start()

    def wait(item):
        for copy in fetches(item, tile_refs[0], 0):
            copy.wait()

    def add_product(item, half):
        sums[half] += jnp.dot(pieces[item], blocks[item], preferred_element_type=jnp.float32)

    for item in range(16):
        start(item, tile_refs[item // 4], item % 4)
    sums[:SPAN] = jnp.zeros((SPAN,) + sums.shape[1:], jnp.float32)
    count = jnp.int32(0)
    for group in range(4):
        for item in range(group * 4, group * 4 + 4):
            wait(item)
        for item in range(group * 4, group * 4 + 4):
            add_product(item, table[0, item] // SPAN)
        for inner in range(4):
            item = 16 + group * 4 + inner
            live = table[0, item] < DEAD

            @pl.when(live)
            def _(item=item, inner=inner, group=group, count=count):
                start(item, tile_refs[4 + group], inner)
                order[count] = item
                target[count] = table[0, item] // SPAN

            count = count + live.astype(jnp.int32)
    for spare in range(3):
        order[count + spare] = 0
        target[count + spare] = SPAN

    def batch(step, carry):
        for lane in range(4):
            place = step * 4 + lane

            @pl.when(place < count)
            def _(place=place):
                wait(order[place])

        for lane in range(4):
            add_product(order[step * 4 + lane], target[step * 4 + lane])
        return carry

    lax.fori_loop(0, (count + 3) // 4, batch, 0)
    mine = table[2, 0]
    outs = []
    total = jnp.zeros((1, sums.shape[2]), jnp.float32)
    for at, (half, out) in enumerate(((1 - mine, send), (mine, keep))):
        value = sums[half]
        value = value * value
        sums[half] = value
        outs.append(pltpu.make_async_copy(sums.at[half], out, out_sem.at[at]))
        outs[-1].start()
        total = total + jnp.sum(value, axis=0, keepdims=True)
    spread[...] = jnp.broadcast_to(total[None], spread.shape)
    outs.append(pltpu.make_async_copy(spread, mass, out_sem.at[2]))
    outs[-1].start()
    for copy in outs:
        copy.wait()


def local(a_tiles, a_where, a_count, b_slab):
    layers = lax.axis_size("layer")
    grid_size = lax.axis_size("col")
    row = lax.axis_index("row")
    col = lax.axis_index("col")
    layer = lax.axis_index("layer")
    slots, tile_size = a_tiles.shape[2], a_tiles.shape[-1]
    slab_cols = b_slab.shape[-1]
    rows = tile_size // layers

    slab_half = lax.dynamic_slice(b_slab[0, 0], (layer * tile_size, 0), (tile_size, slab_cols))
    slab = lax.all_gather(slab_half, ("row", "layer"), axis=0, tiled=True)

    live = jnp.arange(slots, dtype=jnp.int32) < a_count[0, 0]
    codes = jnp.where(live, a_where[0, 0], DEAD).astype(jnp.bfloat16)
    lines = []
    steps = (((0, 1), (1, 0)), ((1, 0), (0, 1)))
    for slot, (first, second) in enumerate(steps):
        piece = lax.dynamic_slice(a_tiles[0, 0], (slot, layer * rows, 0), (1, rows, tile_size))[0]
        code = jnp.broadcast_to(codes[slot], (PAD, tile_size))
        lines.append(gather_line(jnp.concatenate([piece, code], 0), first, layers))
    tiles = []
    for (first, second), line in zip(steps, lines):
        tiles += gather_line(jnp.concatenate(line, 0), second, layers)

    sign = 1 - 2 * layer
    offset = jnp.array([0, -1, 1, -2], jnp.int32) * sign
    here_x, here_y = col // SIDE, col % SIDE
    far_x, far_y = (here_x + offset) % SIDE, (here_y + offset) % SIDE
    source = jnp.stack([far_x[:, None] * SIDE + far_y[None, :], far_x[None, :] * SIDE + far_y[:, None]])
    slab_row = (row + source - col) % grid_size
    stride = rows + PAD
    found = jnp.concatenate([t.reshape(4, stride, tile_size)[:, rows, 0] for t in tiles])
    table = jnp.stack(
        [found.astype(jnp.int32), slab_row.reshape(-1), jnp.broadcast_to(layer, (32,))]
    )

    hbm = pl.BlockSpec(memory_space=pl.ANY)
    members = lax.axis_size("row") * layers
    flops = 2 * 32 * rows * tile_size * slab_cols
    keep, send, mass = pl.pallas_call(
        product_kernel,
        out_shape=(
            jax.ShapeDtypeStruct((rows, slab_cols), jnp.float32),
            jax.ShapeDtypeStruct((rows, slab_cols), jnp.float32),
            jax.ShapeDtypeStruct((members, 1, slab_cols), jnp.float32),
        ),
        in_specs=[pl.BlockSpec(memory_space=pltpu.SMEM)] + [hbm] * 9,
        out_specs=(hbm, hbm, hbm),
        scratch_shapes=[
            pltpu.VMEM((32, rows, tile_size), jnp.bfloat16),
            pltpu.VMEM((32, tile_size, slab_cols), jnp.bfloat16),
            pltpu.VMEM((SPAN + 1, rows, slab_cols), jnp.float32),
            pltpu.VMEM((members, 1, slab_cols), jnp.float32),
            pltpu.SMEM((20,), jnp.int32),
            pltpu.SMEM((20,), jnp.int32),
            pltpu.SemaphoreType.DMA((32,)),
            pltpu.SemaphoreType.DMA((32,)),
            pltpu.SemaphoreType.DMA((3,)),
        ],
        compiler_params=pltpu.CompilerParams(vmem_limit_bytes=60 << 20),
        cost_estimate=pl.CostEstimate(flops=flops, bytes_accessed=20 << 20, transcendentals=0),
    )(table, *tiles, slab)

    matrix_order = grid_size * SPAN * tile_size
    parts = lax.all_to_all(mass, ("row", "layer"), 0, 0, tiled=True)
    other = lax.ppermute(send, "layer", [(0, 1), (1, 0)])
    lower = layer == 0
    halves = jnp.where(lower, keep, other), jnp.where(lower, other, keep)
    column_mass = jnp.sum(parts, axis=(0, 1)) / matrix_order
    return jnp.concatenate(halves, 0) / (column_mass + 1e-06)


def solution(mesh):
    in_specs = (
        P("row", "col", None, None, None),
        P("row", "col", None),
        P("row", "col"),
        P("row", "col", None, None),
    )
    out_specs = P(("row", "layer"), "col")
    return jax.shard_map(local, mesh=mesh, in_specs=in_specs, out_specs=out_specs, check_vma=False)
```

profile of v0, /device:TPU:2, one launch (start us, length us, event | category | flops | bytes accessed | tf_op | source)
XLA Modules:
  0.0 141.1 jit_solution(2374852930150185467)
XLA Ops:
  6.5 1.1 copy-done
  7.7 0.8 constant_dynamic-slice_fusion
  9.1 0.6 fusion.6
  9.7 1.1 constant_dynamic-update-slice_fusion.9
  10.8 0.7 concatenate.43
  11.6 3.5 %collective-permute-start = (bf16[272,512]{1,0:T(8,128)(2,1)S(1)}, bf16[272,512]{1,0:T(8,128)(2,1)S(1)}, u32[]{:S(2)}, u32[]{:S(2)}) collective-permute-start(bf16[272,512]{1,0:T(8,128)(2,1)S(1)} %concatenate.43), channel_id=1, source_target_pairs={{0,2},{1,7},{2,4},{3,1},{4,6},{5,3},{6,0},{7,5},{8,10},{9,15},{10,... | collective-permute-start | bytes 835592 | tf_op jit(solution)/shard_map/ppermute | solution.py:27
  15.0 0.6 concatenate.49
  15.6 3.4 %collective-permute-start.6 = (bf16[272,512]{1,0:T(8,128)(2,1)S(1)}, bf16[272,512]{1,0:T(8,128)(2,1)S(1)}, u32[]{:S(2)}, u32[]{:S(2)}) collective-permute-start(bf16[272,512]{1,0:T(8,128)(2,1)S(1)} %concatenate.49), channel_id=1, source_target_pairs={{0,8},{1,25},{2,10},{3,27},{4,12},{5,29},{6,14},{7,31},{8,16},{9,1... | collective-permute-start | bytes 835592 | tf_op jit(solution)/shard_map/ppermute | solution.py:27
  19.0 3.6 %collective-permute-start.1 = (bf16[272,512]{1,0:T(8,128)(2,1)S(1)}, bf16[272,512]{1,0:T(8,128)(2,1)S(1)}, u32[]{:S(2)}, u32[]{:S(2)}) collective-permute-start(bf16[272,512]{1,0:T(8,128)(2,1)S(1)} %concatenate.43), channel_id=1, source_target_pairs={{0,6},{1,3},{2,0},{3,5},{4,2},{5,7},{6,4},{7,1},{8,14},{9,11},{10,... | collective-permute-start | bytes 835592 | tf_op jit(solution)/shard_map/ppermute | solution.py:27
  22.6 6.3 %collective-permute-start.7 = (bf16[272,512]{1,0:T(8,128)(2,1)S(1)}, bf16[272,512]{1,0:T(8,128)(2,1)S(1)}, u32[]{:S(2)}, u32[]{:S(2)}) collective-permute-start(bf16[272,512]{1,0:T(8,128)(2,1)S(1)} %concatenate.49), channel_id=1, source_target_pairs={{0,24},{1,9},{2,26},{3,11},{4,28},{5,13},{6,30},{7,15},{8,0},{9,17... | collective-permute-start | bytes 835592 | tf_op jit(solution)/shard_map/ppermute | solution.py:27
  28.9 1.2 constant_dynamic-update-slice_fusion.3
  30.2 1.9 %collective-permute-start.2 = (bf16[272,512]{1,0:T(8,128)(2,1)S(1)}, bf16[272,512]{1,0:T(8,128)(2,1)S(1)}, u32[]{:S(2)}, u32[]{:S(2)}) collective-permute-start(bf16[272,512]{1,0:T(8,128)(2,1)S(1)} %collective-permute-done), channel_id=1, source_target_pairs={{0,2},{1,7},{2,4},{3,1},{4,6},{5,3},{6,0},{7,5},{8,10},{9,15},{10,... | collective-permute-start | bytes 835592 | tf_op jit(solution)/shard_map/ppermute | solution.py:27
  32.1 1.9 %collective-permute-start.8 = (bf16[272,512]{1,0:T(8,128)(2,1)S(1)}, bf16[272,512]{1,0:T(8,128)(2,1)S(1)}, u32[]{:S(2)}, u32[]{:S(2)}) collective-permute-start(bf16[272,512]{1,0:T(8,128)(2,1)S(1)} %collective-permute-done.6), channel_id=1, source_target_pairs={{0,8},{1,25},{2,10},{3,27},{4,12},{5,29},{6,14},{7,31},{8,16},{9,1... | collective-permute-start | bytes 835592 | tf_op jit(solution)/shard_map/ppermute | solution.py:27
  34.2 7.6 %collective-permute-done.8 = bf16[272,512]{1,0:T(8,128)(2,1)S(1)} collective-permute-done((bf16[272,512]{1,0:T(8,128)(2,1)S(1)}, bf16[272,512]{1,0:T(8,128)(2,1)S(1)}, u32[]{:S(2)}, u32[]{:S(2)}) %collective-permute-start.8) | collective-permute-done | bytes 278560 | tf_op jit(solution)/shard_map/ppermute | solution.py:27
  41.8 1.9 %collective-permute-start.9 = (bf16[1088,512]{1,0:T(8,128)(2,1)S(1)}, bf16[1088,512]{1,0:T(8,128)(2,1)}, u32[]{:S(2)}, u32[]{:S(2)}) collective-permute-start(bf16[1088,512]{1,0:T(8,128)(2,1)S(1)} %constant_dynamic-update-slice_fusion.5.refs_4_), channel_id=1, source_target_pairs={{0,2},{1,7},{2,4},{3,1},{4,6},{5,3},{6,0},{7,5},{8,10},{9,15},{10,... | collective-permute-start | bytes 3342344 | tf_op jit(solution)/shard_map/ppermute | solution.py:27
  43.8 1.9 %collective-permute-start.3 = (bf16[1088,512]{1,0:T(8,128)(2,1)S(1)}, bf16[1088,512]{1,0:T(8,128)(2,1)}, u32[]{:S(2)}, u32[]{:S(2)}) collective-permute-start(bf16[1088,512]{1,0:T(8,128)(2,1)S(1)} %constant_dynamic-update-slice_fusion.refs_0_), channel_id=1, source_target_pairs={{0,8},{1,25},{2,10},{3,27},{4,12},{5,29},{6,14},{7,31},{8,16},{9,1... | collective-permute-start | bytes 3342344 | tf_op jit(solution)/shard_map/ppermute | solution.py:27
  45.7 5.1 %collective-permute-start.10 = (bf16[1088,512]{1,0:T(8,128)(2,1)S(1)}, bf16[1088,512]{1,0:T(8,128)(2,1)}, u32[]{:S(2)}, u32[]{:S(2)}) collective-permute-start(bf16[1088,512]{1,0:T(8,128)(2,1)S(1)} %constant_dynamic-update-slice_fusion.5.refs_4_), channel_id=1, source_target_pairs={{0,6},{1,3},{2,0},{3,5},{4,2},{5,7},{6,4},{7,1},{8,14},{9,11},{10,... | collective-permute-start | bytes 3342344 | tf_op jit(solution)/shard_map/ppermute | solution.py:27
  50.9 5.1 %collective-permute-start.4 = (bf16[1088,512]{1,0:T(8,128)(2,1)S(1)}, bf16[1088,512]{1,0:T(8,128)(2,1)}, u32[]{:S(2)}, u32[]{:S(2)}) collective-permute-start(bf16[1088,512]{1,0:T(8,128)(2,1)S(1)} %constant_dynamic-update-slice_fusion.refs_0_), channel_id=1, source_target_pairs={{0,24},{1,9},{2,26},{3,11},{4,28},{5,13},{6,30},{7,15},{8,0},{9,17... | collective-permute-start | bytes 3342344 | tf_op jit(solution)/shard_map/ppermute | solution.py:27
  56.0 16.3 %collective-permute-done.9.refs_5_ = bf16[1088,512]{1,0:T(8,128)(2,1)} collective-permute-done((bf16[1088,512]{1,0:T(8,128)(2,1)S(1)}, bf16[1088,512]{1,0:T(8,128)(2,1)}, u32[]{:S(2)}, u32[]{:S(2)}) %collective-permute-start.9) | collective-permute-done | bytes 1114144 | tf_op jit(solution)/shard_map/ppermute | solution.py:27
  72.3 1.9 %collective-permute-start.11 = (bf16[1088,512]{1,0:T(8,128)(2,1)}, bf16[1088,512]{1,0:T(8,128)(2,1)}, u32[]{:S(2)}, u32[]{:S(2)}) collective-permute-start(bf16[1088,512]{1,0:T(8,128)(2,1)} %collective-permute-done.9.refs_5_), channel_id=1, source_target_pairs={{0,2},{1,7},{2,4},{3,1},{4,6},{5,3},{6,0},{7,5},{8,10},{9,15},{10,... | collective-permute-start | bytes 3342344 | tf_op jit(solution)/shard_map/ppermute | solution.py:27
  74.2 1.9 %collective-permute-start.5 = (bf16[1088,512]{1,0:T(8,128)(2,1)}, bf16[1088,512]{1,0:T(8,128)(2,1)}, u32[]{:S(2)}, u32[]{:S(2)}) collective-permute-start(bf16[1088,512]{1,0:T(8,128)(2,1)} %collective-permute-done.3.refs_1_), channel_id=1, source_target_pairs={{0,8},{1,25},{2,10},{3,27},{4,12},{5,29},{6,14},{7,31},{8,16},{9,1... | collective-permute-start | bytes 3342344 | tf_op jit(solution)/shard_map/ppermute | solution.py:27
  76.2 0.1 pad.6.clone
  76.4 0.1 sub.27
  76.5 0.1 copy.14
  76.6 0.1 copy.18
  76.7 0.7 slice.46
  77.4 0.1 copy.20
  77.5 0.7 slice.45
  78.2 0.1 copy.19
  78.3 0.7 slice.42
  79.0 0.1 copy.16
  79.1 0.7 slice.41
  79.8 0.1 copy.15
  80.0 11.3 %collective-permute-done.11.refs_7_ = bf16[1088,512]{1,0:T(8,128)(2,1)} collective-permute-done((bf16[1088,512]{1,0:T(8,128)(2,1)}, bf16[1088,512]{1,0:T(8,128)(2,1)}, u32[]{:S(2)}, u32[]{:S(2)}) %collective-permute-start.11) | collective-permute-done | bytes 1114144 | tf_op jit(solution)/shard_map/ppermute | solution.py:27
  91.2 0.7 slice.47
  91.9 0.1 copy.21
  92.0 0.6 collective-permute-done.5.refs_3_
  92.6 0.7 slice.43
  93.3 0.1 copy.17
  93.4 0.1 concatenate.55
  93.5 0.6 add_add_fusion.1.table
  94.2 6.8 %all-gather.3.cloned.1.call-done = bf16[1,1,16384,384]{3,2,1,0:T(8,128)(2,1)} async-done(((bf16[1,1,512,384]{3,2,1,0:T(8,128)(2,1)}), bf16[1,1,16384,384]{3,2,1,0:T(8,128)(2,1)}) %all-gather.3.cloned.1.call-update) | async-done | bytes 12582928 | tf_op jit(solution)/shard_map/all_gather | solution.py:128
  100.9 9.7 %shard_map.55 = (f32[256,384]{1,0:T(8,128)}, f32[256,384]{1,0:T(8,128)}, f32[32,1,384]{2,1,0:T(1,128)}) custom-call(s32[3,32]{1,0:T(4,128)} %add_add_fusion.1.table, bf16[1088,512]{1,0:T(8,128)(2,1)} %copy-done.2, bf16[1088,512]{1,0:T(8,128)(2,1)} %collective-permute-done.3.refs_1_, bf16[1088,512]{1,0:T(8,128)(2,1)} %collective-permute-done.4.refs_2_, ...), custom_call_target="tpu_custom_call" | custom-call | flops 3221225472 | bytes 20971520 | tf_op jit(solution)/shard_map/pallas_call | solution.py:157
  110.6 7.9 %all-to-all-start = ((f32[32,1,384]{2,1,0:T(1,128)}), f32[32,1,384]{2,1,0:T(1,128)S(1)}, u32[]{:S(2)}, u32[]{:S(2)}) async-start(f32[32,1,384]{2,1,0:T(1,128)} %get-tuple-element.10), calls=%async_computation | async-start | bytes 98304 | tf_op jit(solution)/shard_map/all_to_all | solution.py:182
  118.5 2.2 %collective-permute-start.12 = (f32[256,384]{1,0:T(8,128)}, f32[256,384]{1,0:T(8,128)S(1)}, u32[]{:S(2)}, u32[]{:S(2)}) collective-permute-start(f32[256,384]{1,0:T(8,128)} %get-tuple-element.9), channel_id=1, source_target_pairs={{0,1},{1,0},{2,3},{3,2},{4,5},{5,4},{6,7},{7,6},{8,9},{9,8},{10,11... | collective-permute-start | bytes 1179656 | tf_op jit(solution)/shard_map/ppermute | solution.py:183
  120.7 11.5 %all-to-all-done = f32[32,1,384]{2,1,0:T(1,128)S(1)} async-done(((f32[32,1,384]{2,1,0:T(1,128)}), f32[32,1,384]{2,1,0:T(1,128)S(1)}, u32[]{:S(2)}, u32[]{:S(2)}) %all-to-all-start) | async-done | bytes 49184 | tf_op jit(solution)/shard_map/all_to_all | solution.py:182
  132.3 1.1 broadcast_select_fusion.1
  133.3 0.9 maximum_divide_fusion
  (36 shorter events, 0.4 us)
Async XLA Ops:
  6.5 1.1 copy-start
  6.5 2.6 %copy-start.4 = (s32[1,1,2]{2,1,0:T(1,128)S(1)}, s32[1,1,2]{2,1,0:T(1,128)}, u32[]{:S(2)}) copy-start(s32[1,1,2]{2,1,0:T(1,128)} %param.6) | copy-start | bytes 28
  6.5 94.4 %all-gather.3.cloned.1.call-start = ((), (), s32[]{:S(2)}) async-start(), calls=%async_computation.1 | async-start | bytes 12976128 | tf_op jit(solution)/shard_map/all_gather | solution.py:128
  11.6 18.6 %collective-permute-start = (bf16[272,512]{1,0:T(8,128)(2,1)S(1)}, bf16[272,512]{1,0:T(8,128)(2,1)S(1)}, u32[]{:S(2)}, u32[]{:S(2)}) collective-permute-start(bf16[272,512]{1,0:T(8,128)(2,1)S(1)} %concatenate.43), channel_id=1, source_target_pairs={{0,2},{1,7},{2,4},{3,1},{4,6},{5,3},{6,0},{7,5},{8,10},{9,15},{10,... | collective-permute-start | bytes 835592 | tf_op jit(solution)/shard_map/ppermute | solution.py:27
  15.6 16.5 %collective-permute-start.6 = (bf16[272,512]{1,0:T(8,128)(2,1)S(1)}, bf16[272,512]{1,0:T(8,128)(2,1)S(1)}, u32[]{:S(2)}, u32[]{:S(2)}) collective-permute-start(bf16[272,512]{1,0:T(8,128)(2,1)S(1)} %concatenate.49), channel_id=1, source_target_pairs={{0,8},{1,25},{2,10},{3,27},{4,12},{5,29},{6,14},{7,31},{8,16},{9,1... | collective-permute-start | bytes 835592 | tf_op jit(solution)/shard_map/ppermute | solution.py:27
  19.0 15.1 %collective-permute-start.1 = (bf16[272,512]{1,0:T(8,128)(2,1)S(1)}, bf16[272,512]{1,0:T(8,128)(2,1)S(1)}, u32[]{:S(2)}, u32[]{:S(2)}) collective-permute-start(bf16[272,512]{1,0:T(8,128)(2,1)S(1)} %concatenate.43), channel_id=1, source_target_pairs={{0,6},{1,3},{2,0},{3,5},{4,2},{5,7},{6,4},{7,1},{8,14},{9,11},{10,... | collective-permute-start | bytes 835592 | tf_op jit(solution)/shard_map/ppermute | solution.py:27
  22.6 11.6 %collective-permute-start.7 = (bf16[272,512]{1,0:T(8,128)(2,1)S(1)}, bf16[272,512]{1,0:T(8,128)(2,1)S(1)}, u32[]{:S(2)}, u32[]{:S(2)}) collective-permute-start(bf16[272,512]{1,0:T(8,128)(2,1)S(1)} %concatenate.49), channel_id=1, source_target_pairs={{0,24},{1,9},{2,26},{3,11},{4,28},{5,13},{6,30},{7,15},{8,0},{9,17... | collective-permute-start | bytes 835592 | tf_op jit(solution)/shard_map/ppermute | solution.py:27
  30.2 13.6 %collective-permute-start.2 = (bf16[272,512]{1,0:T(8,128)(2,1)S(1)}, bf16[272,512]{1,0:T(8,128)(2,1)S(1)}, u32[]{:S(2)}, u32[]{:S(2)}) collective-permute-start(bf16[272,512]{1,0:T(8,128)(2,1)S(1)} %collective-permute-done), channel_id=1, source_target_pairs={{0,2},{1,7},{2,4},{3,1},{4,6},{5,3},{6,0},{7,5},{8,10},{9,15},{10,... | collective-permute-start | bytes 835592 | tf_op jit(solution)/shard_map/ppermute | solution.py:27
  32.1 9.7 %collective-permute-start.8 = (bf16[272,512]{1,0:T(8,128)(2,1)S(1)}, bf16[272,512]{1,0:T(8,128)(2,1)S(1)}, u32[]{:S(2)}, u32[]{:S(2)}) collective-permute-start(bf16[272,512]{1,0:T(8,128)(2,1)S(1)} %collective-permute-done.6), channel_id=1, source_target_pairs={{0,8},{1,25},{2,10},{3,27},{4,12},{5,29},{6,14},{7,31},{8,16},{9,1... | collective-permute-start | bytes 835592 | tf_op jit(solution)/shard_map/ppermute | solution.py:27
  34.1 42.2 %copy-start.3 = (s32[4]{0:T(128)S(1)}, s32[4]{0:T(128)}, u32[]{:S(2)}) copy-start(s32[4]{0:T(128)} %constant.88.clone) | copy-start | bytes 52
  41.8 59.1 %copy-start.1 = (bf16[1088,512]{1,0:T(8,128)(2,1)}, bf16[1088,512]{1,0:T(8,128)(2,1)S(1)}, u32[]{:S(2)}) copy-start(bf16[1088,512]{1,0:T(8,128)(2,1)S(1)} %constant_dynamic-update-slice_fusion.5.refs_4_) | copy-start | bytes 3342340
  41.8 30.5 %collective-permute-start.9 = (bf16[1088,512]{1,0:T(8,128)(2,1)S(1)}, bf16[1088,512]{1,0:T(8,128)(2,1)}, u32[]{:S(2)}, u32[]{:S(2)}) collective-permute-start(bf16[1088,512]{1,0:T(8,128)(2,1)S(1)} %constant_dynamic-update-slice_fusion.5.refs_4_), channel_id=1, source_target_pairs={{0,2},{1,7},{2,4},{3,1},{4,6},{5,3},{6,0},{7,5},{8,10},{9,15},{10,... | collective-permute-start | bytes 3342344 | tf_op jit(solution)/shard_map/ppermute | solution.py:27
  43.8 57.1 %copy-start.2 = (bf16[1088,512]{1,0:T(8,128)(2,1)}, bf16[1088,512]{1,0:T(8,128)(2,1)S(1)}, u32[]{:S(2)}) copy-start(bf16[1088,512]{1,0:T(8,128)(2,1)S(1)} %constant_dynamic-update-slice_fusion.refs_0_) | copy-start | bytes 3342340
  43.8 30.4 %collective-permute-start.3 = (bf16[1088,512]{1,0:T(8,128)(2,1)S(1)}, bf16[1088,512]{1,0:T(8,128)(2,1)}, u32[]{:S(2)}, u32[]{:S(2)}) collective-permute-start(bf16[1088,512]{1,0:T(8,128)(2,1)S(1)} %constant_dynamic-update-slice_fusion.refs_0_), channel_id=1, source_target_pairs={{0,8},{1,25},{2,10},{3,27},{4,12},{5,29},{6,14},{7,31},{8,16},{9,1... | collective-permute-start | bytes 3342344 | tf_op jit(solution)/shard_map/ppermute | solution.py:27
  45.7 31.0 %collective-permute-start.10 = (bf16[1088,512]{1,0:T(8,128)(2,1)S(1)}, bf16[1088,512]{1,0:T(8,128)(2,1)}, u32[]{:S(2)}, u32[]{:S(2)}) collective-permute-start(bf16[1088,512]{1,0:T(8,128)(2,1)S(1)} %constant_dynamic-update-slice_fusion.5.refs_4_), channel_id=1, source_target_pairs={{0,6},{1,3},{2,0},{3,5},{4,2},{5,7},{6,4},{7,1},{8,14},{9,11},{10,... | collective-permute-start | bytes 3342344 | tf_op jit(solution)/shard_map/ppermute | solution.py:27
  50.9 27.4 %collective-permute-start.4 = (bf16[1088,512]{1,0:T(8,128)(2,1)S(1)}, bf16[1088,512]{1,0:T(8,128)(2,1)}, u32[]{:S(2)}, u32[]{:S(2)}) collective-permute-start(bf16[1088,512]{1,0:T(8,128)(2,1)S(1)} %constant_dynamic-update-slice_fusion.refs_0_), channel_id=1, source_target_pairs={{0,24},{1,9},{2,26},{3,11},{4,28},{5,13},{6,30},{7,15},{8,0},{9,17... | collective-permute-start | bytes 3342344 | tf_op jit(solution)/shard_map/ppermute | solution.py:27
  72.3 18.9 %collective-permute-start.11 = (bf16[1088,512]{1,0:T(8,128)(2,1)}, bf16[1088,512]{1,0:T(8,128)(2,1)}, u32[]{:S(2)}, u32[]{:S(2)}) collective-permute-start(bf16[1088,512]{1,0:T(8,128)(2,1)} %collective-permute-done.9.refs_5_), channel_id=1, source_target_pairs={{0,2},{1,7},{2,4},{3,1},{4,6},{5,3},{6,0},{7,5},{8,10},{9,15},{10,... | collective-permute-start | bytes 3342344 | tf_op jit(solution)/shard_map/ppermute | solution.py:27
  74.2 18.3 %collective-permute-start.5 = (bf16[1088,512]{1,0:T(8,128)(2,1)}, bf16[1088,512]{1,0:T(8,128)(2,1)}, u32[]{:S(2)}, u32[]{:S(2)}) collective-permute-start(bf16[1088,512]{1,0:T(8,128)(2,1)} %collective-permute-done.3.refs_1_), channel_id=1, source_target_pairs={{0,8},{1,25},{2,10},{3,27},{4,12},{5,29},{6,14},{7,31},{8,16},{9,1... | collective-permute-start | bytes 3342344 | tf_op jit(solution)/shard_map/ppermute | solution.py:27
  110.6 21.6 %all-to-all-start = ((f32[32,1,384]{2,1,0:T(1,128)}), f32[32,1,384]{2,1,0:T(1,128)S(1)}, u32[]{:S(2)}, u32[]{:S(2)}) async-start(f32[32,1,384]{2,1,0:T(1,128)} %get-tuple-element.10), calls=%async_computation | async-start | bytes 98304 | tf_op jit(solution)/shard_map/all_to_all | solution.py:182
  118.5 13.7 %collective-permute-start.12 = (f32[256,384]{1,0:T(8,128)}, f32[256,384]{1,0:T(8,128)S(1)}, u32[]{:S(2)}, u32[]{:S(2)}) collective-permute-start(f32[256,384]{1,0:T(8,128)} %get-tuple-element.9), channel_id=1, source_target_pairs={{0,1},{1,0},{2,3},{3,2},{4,5},{5,4},{6,7},{7,6},{8,9},{9,8},{10,11... | collective-permute-start | bytes 1179656 | tf_op jit(solution)/shard_map/ppermute | solution.py:183
Sparse Core Ops, SparseCore 0:
  9.5 91.4 all-gather.2
where the time goes:
time: 142 us; the launch traced here: 141 us
  waiting for transfers between devices  54 us (38%)
  starting transfers between devices  48.7 us (34%)
  between operations  14.4 us (10%)
  local copies, waits for them, and re-layouts  11.6 us (8%)
  Pallas kernels  9.65 us (7%)
  other arithmetic  2.82 us (2%)
    ppermute x12, starting transfers between devices, shift(): lax.ppermute(value, ('col', 'layer'), torus_pairs((sign * step[0], sign *...  38.5 us
    ppermute x12, waiting for transfers between devices, shift(): lax.ppermute(value, ('col', 'layer'), torus_pairs((sign * step[0], sign *...  35.7 us
    all_to_all x1, waiting for transfers between devices, local(): parts = lax.all_to_all(mass, ('row', 'layer'), 0, 0, tiled=True)  11.5 us
    pallas_call x1, Pallas kernels, local(): pl.pallas_call(product_kernel, out_shape=(jax.ShapeDtypeStruct((rows, sla...  9.65 us
    all_to_all x1, starting transfers between devices, local(): parts = lax.all_to_all(mass, ('row', 'layer'), 0, 0, tiled=True)  7.93 us
    all_gather x1, waiting for transfers between devices, local(): slab = lax.all_gather(slab_half, ('row', 'layer'), axis=0, tiled=True)  6.78 us
    unnamed x24, local copies, waits for them, and re-layouts  4.44 us
    slice x8, local copies, waits for them, and re-layouts, local(): t.reshape(4, stride, tile_size)[:, rows, 0]  4.22 us
  transfers between devices with their start and end apart: 15, of which 6 were waited for; matrix products, arithmetic and copies ran while one was open for 7% of the time, Pallas kernels for 0%

commit v1 on v0

--- a/solution.py
+++ b/solution.py
@@ -35,53 +35,51 @@
 
 def product_kernel(table, *refs):
     tile_refs = refs[:8]
-    slab, keep, send, mass, pieces, blocks, sums, spread, order, target = refs[8:18]
-    piece_sem, block_sem, out_sem = refs[18:]
+    slab, keep, send, mass, pieces, blocks, sums, spread, order, target, source = refs[8:19]
+    piece_sem, block_sem, out_sem = refs[19:]
     rows, depth = pieces.shape[1], blocks.shape[1]
     stride = rows + PAD
 
-    def fetches(item, tiles, inner):
+    def fetch_piece(item, tiles, inner):
+        first = pl.multiple_of(inner * stride, PAD)
+        return pltpu.make_async_copy(tiles.at[pl.ds(first, rows), :], pieces.at[item], piece_sem.at[item])
+
+    def fetch_block(item):
         block = table[1, item] * SPAN + table[0, item] % SPAN
-        start = pl.multiple_of(block * depth, depth)
-        first = pl.multiple_of(inner * stride, PAD)
-        return (
-            pltpu.make_async_copy(tiles.at[pl.ds(first, rows), :], pieces.at[item], piece_sem.at[item]),
-            pltpu.make_async_copy(slab.at[pl.ds(start, depth), :], blocks.at[item], block_sem.at[item]),
-        )
-
-    def start(item, tiles, inner):
-        for copy in fetches(item, tiles, inner):
-            copy.start()
-
-    def wait(item):
-        for copy in fetches(item, tile_refs[0], 0):
-            copy.wait()
-
-    def add_product(item, half):
-        sums[half] += jnp.dot(pieces[item], blocks[item], preferred_element_type=jnp.float32)
+        first = pl.multiple_of(block * depth, depth)
+        return pltpu.make_async_copy(slab.at[pl.ds(first, depth), :], blocks.at[item], block_sem.at[item])
+
+    def add_product(item, block, half):
+        sums[half] += jnp.dot(pieces[item], blocks[block], preferred_element_type=jnp.float32)
 
     for item in range(16):
-        start(item, tile_refs[item // 4], item % 4)
+        fetch_piece(item, tile_refs[item // 4], item % 4).start()
+        fetch_block(item).start()
     sums[:SPAN] = jnp.zeros((SPAN,) + sums.shape[1:], jnp.float32)
     count = jnp.int32(0)
     for group in range(4):
         for item in range(group * 4, group * 4 + 4):
-            wait(item)
+            fetch_piece(item, tile_refs[0], 0).wait()
+            fetch_block(item).wait()
         for item in range(group * 4, group * 4 + 4):
-            add_product(item, table[0, item] // SPAN)
+            add_product(item, item, table[0, item] // SPAN)
         for inner in range(4):
-            item = 16 + group * 4 + inner
+            item, mate = 16 + group * 4 + inner, inner * 4 + group
             live = table[0, item] < DEAD
+            own = table[0, item] % SPAN != table[0, mate] % SPAN
 
             @pl.when(live)
-            def _(item=item, inner=inner, group=group, count=count):
-                start(item, tile_refs[4 + group], inner)
+            def _(item=item, inner=inner, group=group, count=count, own=own, mate=mate):
+                fetch_piece(item, tile_refs[4 + group], inner).start()
+                pl.when(own)(lambda: fetch_block(item).start())
                 order[count] = item
+                source[count] = jnp.where(own, item, mate)
                 target[count] = table[0, item] // SPAN
 
             count = count + live.astype(jnp.int32)
     for spare in range(3):
         order[count + spare] = 0
+        source[count + spare] = 0
         target[count + spare] = SPAN
 
     def batch(step, carry):
@@ -90,10 +88,13 @@
 
             @pl.when(place < count)
             def _(place=place):
-                wait(order[place])
+                item = order[place]
+                fetch_piece(item, tile_refs[0], 0).wait()
+                pl.when(source[place] == item)(lambda: fetch_block(item).wait())
 
         for lane in range(4):
-            add_product(order[step * 4 + lane], target[step * 4 + lane])
+            place = step * 4 + lane
+            add_product(order[place], source[place], target[place])
         return carry
 
     lax.fori_loop(0, (count + 3) // 4, batch, 0)
@@ -157,9 +158,9 @@
     keep, send, mass = pl.pallas_call(
         product_kernel,
         out_shape=(
-            jax.ShapeDtypeStruct((rows, slab_cols), jnp.float32),
-            jax.ShapeDtypeStruct((rows, slab_cols), jnp.float32),
-            jax.ShapeDtypeStruct((members, 1, slab_cols), jnp.float32),
+            pltpu.HBM((rows, slab_cols), jnp.float32),
+            pltpu.HBM((rows, slab_cols), jnp.float32),
+            pltpu.HBM((members, 1, slab_cols), jnp.float32),
         ),
         in_specs=[pl.BlockSpec(memory_space=pltpu.SMEM)] + [hbm] * 9,
         out_specs=(hbm, hbm, hbm),
@@ -170,11 +171,12 @@
             pltpu.VMEM((members, 1, slab_cols), jnp.float32),
             pltpu.SMEM((20,), jnp.int32),
             pltpu.SMEM((20,), jnp.int32),
+            pltpu.SMEM((20,), jnp.int32),
             pltpu.SemaphoreType.DMA((32,)),
             pltpu.SemaphoreType.DMA((32,)),
             pltpu.SemaphoreType.DMA((3,)),
         ],
-        compiler_params=pltpu.CompilerParams(vmem_limit_bytes=60 << 20),
+        compiler_params=pltpu.CompilerParams(vmem_limit_bytes=44 << 20),
         cost_estimate=pl.CostEstimate(flops=flops, bytes_accessed=20 << 20, transcendentals=0),
     )(table, *tiles, slab)
 

time: 142 us -> 141 us (level)
  the two profiles are of different devices: /device:TPU:2 before, /device:TPU:18 now
where the time goes in v1:
time: 141 us; the launch traced here: 140 us
  waiting for transfers between devices  55.1 us (39%)
  starting transfers between devices  48.1 us (34%)
  between operations  14.4 us (10%)
  local copies, waits for them, and re-layouts  11.5 us (8%)
  Pallas kernels  8.82 us (6%)
  other arithmetic  2.25 us (2%)
    ppermute x12, starting transfers between devices, shift(): lax.ppermute(value, ('col', 'layer'), torus_pairs((sign * step[0], sign *...  38 us
    ppermute x12, waiting for transfers between devices, shift(): lax.ppermute(value, ('col', 'layer'), torus_pairs((sign * step[0], sign *...  36 us
    all_to_all x1, waiting for transfers between devices, local(): parts = lax.all_to_all(mass, ('row', 'layer'), 0, 0, tiled=True)  11.5 us
    pallas_call x1, Pallas kernels, local(): pl.pallas_call(product_kernel, out_shape=(pltpu.HBM((rows, slab_cols), jn...  8.82 us
    all_to_all x1, starting transfers between devices, local(): parts = lax.all_to_all(mass, ('row', 'layer'), 0, 0, tiled=True)  7.88 us
    all_gather x1, waiting for transfers between devices, local(): slab = lax.all_gather(slab_half, ('row', 'layer'), axis=0, tiled=True)  7.66 us
    unnamed x20, local copies, waits for them, and re-layouts  4.39 us
    slice x8, local copies, waits for them, and re-layouts, local(): t.reshape(4, stride, tile_size)[:, rows, 0]  4.23 us
  transfers between devices with their start and end apart: 15, of which 7 were waited for; matrix products, arithmetic and copies ran while one was open for 7% of the time, Pallas kernels for 0%

profile of v1, /device:TPU:18, one launch (start us, length us, event | category | flops | bytes accessed | tf_op | source)
XLA Modules:
  0.0 140.2 jit_solution(14060699733264645964)
XLA Ops:
  6.5 1.1 copy-done
  7.7 0.8 constant_dynamic-slice_fusion
  9.1 0.6 fusion.6
  9.7 1.1 constant_dynamic-update-slice_fusion.9
  10.8 0.7 concatenate.43
  11.5 3.2 %collective-permute-start = (bf16[272,512]{1,0:T(8,128)(2,1)S(1)}, bf16[272,512]{1,0:T(8,128)(2,1)S(1)}, u32[]{:S(2)}, u32[]{:S(2)}) collective-permute-start(bf16[272,512]{1,0:T(8,128)(2,1)S(1)} %concatenate.43), channel_id=1, source_target_pairs={{0,2},{1,7},{2,4},{3,1},{4,6},{5,3},{6,0},{7,5},{8,10},{9,15},{10,... | collective-permute-start | bytes 835592 | tf_op jit(solution)/shard_map/ppermute | solution.py:27
  14.7 0.6 concatenate.49
  15.3 3.4 %collective-permute-start.6 = (bf16[272,512]{1,0:T(8,128)(2,1)S(1)}, bf16[272,512]{1,0:T(8,128)(2,1)S(1)}, u32[]{:S(2)}, u32[]{:S(2)}) collective-permute-start(bf16[272,512]{1,0:T(8,128)(2,1)S(1)} %concatenate.49), channel_id=1, source_target_pairs={{0,8},{1,25},{2,10},{3,27},{4,12},{5,29},{6,14},{7,31},{8,16},{9,1... | collective-permute-start | bytes 835592 | tf_op jit(solution)/shard_map/ppermute | solution.py:27
  18.7 2.7 %collective-permute-start.1 = (bf16[272,512]{1,0:T(8,128)(2,1)S(1)}, bf16[272,512]{1,0:T(8,128)(2,1)S(1)}, u32[]{:S(2)}, u32[]{:S(2)}) collective-permute-start(bf16[272,512]{1,0:T(8,128)(2,1)S(1)} %concatenate.43), channel_id=1, source_target_pairs={{0,6},{1,3},{2,0},{3,5},{4,2},{5,7},{6,4},{7,1},{8,14},{9,11},{10,... | collective-permute-start | bytes 835592 | tf_op jit(solution)/shard_map/ppermute | solution.py:27
  21.4 2.4 %collective-permute-start.7 = (bf16[272,512]{1,0:T(8,128)(2,1)S(1)}, bf16[272,512]{1,0:T(8,128)(2,1)S(1)}, u32[]{:S(2)}, u32[]{:S(2)}) collective-permute-start(bf16[272,512]{1,0:T(8,128)(2,1)S(1)} %concatenate.49), channel_id=1, source_target_pairs={{0,24},{1,9},{2,26},{3,11},{4,28},{5,13},{6,30},{7,15},{8,0},{9,17... | collective-permute-start | bytes 835592 | tf_op jit(solution)/shard_map/ppermute | solution.py:27
  23.8 1.2 constant_dynamic-update-slice_fusion.3
  25.0 5.3 %collective-permute-start.2 = (bf16[272,512]{1,0:T(8,128)(2,1)S(1)}, bf16[272,512]{1,0:T(8,128)(2,1)S(1)}, u32[]{:S(2)}, u32[]{:S(2)}) collective-permute-start(bf16[272,512]{1,0:T(8,128)(2,1)S(1)} %collective-permute-done), channel_id=1, source_target_pairs={{0,2},{1,7},{2,4},{3,1},{4,6},{5,3},{6,0},{7,5},{8,10},{9,15},{10,... | collective-permute-start | bytes 835592 | tf_op jit(solution)/shard_map/ppermute | solution.py:27
  30.3 1.9 %collective-permute-start.8 = (bf16[272,512]{1,0:T(8,128)(2,1)S(1)}, bf16[272,512]{1,0:T(8,128)(2,1)S(1)}, u32[]{:S(2)}, u32[]{:S(2)}) collective-permute-start(bf16[272,512]{1,0:T(8,128)(2,1)S(1)} %collective-permute-done.6), channel_id=1, source_target_pairs={{0,8},{1,25},{2,10},{3,27},{4,12},{5,29},{6,14},{7,31},{8,16},{9,1... | collective-permute-start | bytes 835592 | tf_op jit(solution)/shard_map/ppermute | solution.py:27
  32.4 7.6 %collective-permute-done.8 = bf16[272,512]{1,0:T(8,128)(2,1)S(1)} collective-permute-done((bf16[272,512]{1,0:T(8,128)(2,1)S(1)}, bf16[272,512]{1,0:T(8,128)(2,1)S(1)}, u32[]{:S(2)}, u32[]{:S(2)}) %collective-permute-start.8) | collective-permute-done | bytes 278560 | tf_op jit(solution)/shard_map/ppermute | solution.py:27
  40.0 5.1 %collective-permute-start.9 = (bf16[1088,512]{1,0:T(8,128)(2,1)S(1)}, bf16[1088,512]{1,0:T(8,128)(2,1)}, u32[]{:S(2)}, u32[]{:S(2)}) collective-permute-start(bf16[1088,512]{1,0:T(8,128)(2,1)S(1)} %constant_dynamic-update-slice_fusion.5.refs_4_), channel_id=1, source_target_pairs={{0,2},{1,7},{2,4},{3,1},{4,6},{5,3},{6,0},{7,5},{8,10},{9,15},{10,... | collective-permute-start | bytes 3342344 | tf_op jit(solution)/shard_map/ppermute | solution.py:27
  45.2 1.9 %collective-permute-start.3 = (bf16[1088,512]{1,0:T(8,128)(2,1)S(1)}, bf16[1088,512]{1,0:T(8,128)(2,1)}, u32[]{:S(2)}, u32[]{:S(2)}) collective-permute-start(bf16[1088,512]{1,0:T(8,128)(2,1)S(1)} %constant_dynamic-update-slice_fusion.refs_0_), channel_id=1, source_target_pairs={{0,8},{1,25},{2,10},{3,27},{4,12},{5,29},{6,14},{7,31},{8,16},{9,1... | collective-permute-start | bytes 3342344 | tf_op jit(solution)/shard_map/ppermute | solution.py:27
  47.1 1.9 %collective-permute-start.10 = (bf16[1088,512]{1,0:T(8,128)(2,1)S(1)}, bf16[1088,512]{1,0:T(8,128)(2,1)}, u32[]{:S(2)}, u32[]{:S(2)}) collective-permute-start(bf16[1088,512]{1,0:T(8,128)(2,1)S(1)} %constant_dynamic-update-slice_fusion.5.refs_4_), channel_id=1, source_target_pairs={{0,6},{1,3},{2,0},{3,5},{4,2},{5,7},{6,4},{7,1},{8,14},{9,11},{10,... | collective-permute-start | bytes 3342344 | tf_op jit(solution)/shard_map/ppermute | solution.py:27
  49.0 5.1 %collective-permute-start.4 = (bf16[1088,512]{1,0:T(8,128)(2,1)S(1)}, bf16[1088,512]{1,0:T(8,128)(2,1)}, u32[]{:S(2)}, u32[]{:S(2)}) collective-permute-start(bf16[1088,512]{1,0:T(8,128)(2,1)S(1)} %constant_dynamic-update-slice_fusion.refs_0_), channel_id=1, source_target_pairs={{0,24},{1,9},{2,26},{3,11},{4,28},{5,13},{6,30},{7,15},{8,0},{9,17... | collective-permute-start | bytes 3342344 | tf_op jit(solution)/shard_map/ppermute | solution.py:27
  54.2 14.5 %collective-permute-done.9.refs_5_ = bf16[1088,512]{1,0:T(8,128)(2,1)} collective-permute-done((bf16[1088,512]{1,0:T(8,128)(2,1)S(1)}, bf16[1088,512]{1,0:T(8,128)(2,1)}, u32[]{:S(2)}, u32[]{:S(2)}) %collective-permute-start.9) | collective-permute-done | bytes 1114144 | tf_op jit(solution)/shard_map/ppermute | solution.py:27
  68.7 3.2 %collective-permute-start.11 = (bf16[1088,512]{1,0:T(8,128)(2,1)}, bf16[1088,512]{1,0:T(8,128)(2,1)}, u32[]{:S(2)}, u32[]{:S(2)}) collective-permute-start(bf16[1088,512]{1,0:T(8,128)(2,1)} %collective-permute-done.9.refs_5_), channel_id=1, source_target_pairs={{0,2},{1,7},{2,4},{3,1},{4,6},{5,3},{6,0},{7,5},{8,10},{9,15},{10,... | collective-permute-start | bytes 3342344 | tf_op jit(solution)/shard_map/ppermute | solution.py:27
  71.8 1.8 %collective-permute-done.3.refs_1_ = bf16[1088,512]{1,0:T(8,128)(2,1)} collective-permute-done((bf16[1088,512]{1,0:T(8,128)(2,1)S(1)}, bf16[1088,512]{1,0:T(8,128)(2,1)}, u32[]{:S(2)}, u32[]{:S(2)}) %collective-permute-start.3) | collective-permute-done | bytes 1114144 | tf_op jit(solution)/shard_map/ppermute | solution.py:27
  73.6 1.9 %collective-permute-start.5 = (bf16[1088,512]{1,0:T(8,128)(2,1)}, bf16[1088,512]{1,0:T(8,128)(2,1)}, u32[]{:S(2)}, u32[]{:S(2)}) collective-permute-start(bf16[1088,512]{1,0:T(8,128)(2,1)} %collective-permute-done.3.refs_1_), channel_id=1, source_target_pairs={{0,8},{1,25},{2,10},{3,27},{4,12},{5,29},{6,14},{7,31},{8,16},{9,1... | collective-permute-start | bytes 3342344 | tf_op jit(solution)/shard_map/ppermute | solution.py:27
  75.5 0.1 pad.6.clone
  75.7 0.1 sub.27
  75.8 0.1 copy.14
  75.9 0.1 copy.18
  76.1 0.7 slice.46
  76.8 0.1 copy.20
  76.9 0.7 slice.45
  77.6 0.1 copy.19
  77.7 0.7 slice.42
  78.4 0.1 copy.16
  78.5 0.7 slice.41
  79.2 0.1 copy.15
  79.3 7.1 %collective-permute-done.11.refs_7_ = bf16[1088,512]{1,0:T(8,128)(2,1)} collective-permute-done((bf16[1088,512]{1,0:T(8,128)(2,1)}, bf16[1088,512]{1,0:T(8,128)(2,1)}, u32[]{:S(2)}, u32[]{:S(2)}) %collective-permute-start.11) | collective-permute-done | bytes 1114144 | tf_op jit(solution)/shard_map/ppermute | solution.py:27
  86.4 0.7 slice.47
  87.1 0.1 copy.21
  87.2 5.1 %collective-permute-done.5.refs_3_ = bf16[1088,512]{1,0:T(8,128)(2,1)} collective-permute-done((bf16[1088,512]{1,0:T(8,128)(2,1)}, bf16[1088,512]{1,0:T(8,128)(2,1)}, u32[]{:S(2)}, u32[]{:S(2)}) %collective-permute-start.5) | collective-permute-done | bytes 1114144 | tf_op jit(solution)/shard_map/ppermute | solution.py:27
  92.2 0.7 slice.43
  92.9 0.1 copy.17
  93.0 0.1 concatenate.55
  93.2 7.7 %all-gather.3.cloned.1.call-done = bf16[1,1,16384,384]{3,2,1,0:T(8,128)(2,1)} async-done(((bf16[1,1,512,384]{3,2,1,0:T(8,128)(2,1)}), bf16[1,1,16384,384]{3,2,1,0:T(8,128)(2,1)}) %all-gather.3.cloned.1.call-update) | async-done | bytes 12582928 | tf_op jit(solution)/shard_map/all_gather | solution.py:129
  100.9 8.8 %shard_map.55 = (f32[256,384]{1,0:T(8,128)}, f32[256,384]{1,0:T(8,128)}, f32[32,1,384]{2,1,0:T(1,128)}) custom-call(s32[3,32]{1,0:T(4,128)S(1)} %add_add_fusion.1.table, bf16[1088,512]{1,0:T(8,128)(2,1)S(1)} %constant_dynamic-update-slice_fusion.refs_0_, bf16[1088,512]{1,0:T(8,128)(2,1)} %collective-permute-done.3.refs_1_, ...), custom_call_target="tpu_custom_call" | custom-call | flops 3221225472 | bytes 20971520 | tf_op jit(solution)/shard_map/pallas_call | solution.py:158
  109.7 7.9 %all-to-all-start = ((f32[32,1,384]{2,1,0:T(1,128)}), f32[32,1,384]{2,1,0:T(1,128)S(1)}, u32[]{:S(2)}, u32[]{:S(2)}) async-start(f32[32,1,384]{2,1,0:T(1,128)} %get-tuple-element.10), calls=%async_computation | async-start | bytes 98304 | tf_op jit(solution)/shard_map/all_to_all | solution.py:184
  117.6 2.2 %collective-permute-start.12 = (f32[256,384]{1,0:T(8,128)}, f32[256,384]{1,0:T(8,128)S(1)}, u32[]{:S(2)}, u32[]{:S(2)}) collective-permute-start(f32[256,384]{1,0:T(8,128)} %get-tuple-element.9), channel_id=1, source_target_pairs={{0,1},{1,0},{2,3},{3,2},{4,5},{5,4},{6,7},{7,6},{8,9},{9,8},{10,11... | collective-permute-start | bytes 1179656 | tf_op jit(solution)/shard_map/ppermute | solution.py:185
  119.8 11.5 %all-to-all-done = f32[32,1,384]{2,1,0:T(1,128)S(1)} async-done(((f32[32,1,384]{2,1,0:T(1,128)}), f32[32,1,384]{2,1,0:T(1,128)S(1)}, u32[]{:S(2)}, u32[]{:S(2)}) %all-to-all-start) | async-done | bytes 49184 | tf_op jit(solution)/shard_map/all_to_all | solution.py:184
  131.4 1.1 broadcast_select_fusion.1
  132.4 0.9 maximum_divide_fusion
  (32 shorter events, 0.4 us)
Async XLA Ops:
  6.5 1.1 copy-start
  6.5 2.6 %copy-start.2 = (s32[1,1,2]{2,1,0:T(1,128)S(1)}, s32[1,1,2]{2,1,0:T(1,128)}, u32[]{:S(2)}) copy-start(s32[1,1,2]{2,1,0:T(1,128)} %param.6) | copy-start | bytes 28
  6.5 94.4 %all-gather.3.cloned.1.call-start = ((), (), s32[]{:S(2)}) async-start(), calls=%async_computation.1 | async-start | bytes 12976128 | tf_op jit(solution)/shard_map/all_gather | solution.py:129
  11.5 13.5 %collective-permute-start = (bf16[272,512]{1,0:T(8,128)(2,1)S(1)}, bf16[272,512]{1,0:T(8,128)(2,1)S(1)}, u32[]{:S(2)}, u32[]{:S(2)}) collective-permute-start(bf16[272,512]{1,0:T(8,128)(2,1)S(1)} %concatenate.43), channel_id=1, source_target_pairs={{0,2},{1,7},{2,4},{3,1},{4,6},{5,3},{6,0},{7,5},{8,10},{9,15},{10,... | collective-permute-start | bytes 835592 | tf_op jit(solution)/shard_map/ppermute | solution.py:27
  15.3 15.0 %collective-permute-start.6 = (bf16[272,512]{1,0:T(8,128)(2,1)S(1)}, bf16[272,512]{1,0:T(8,128)(2,1)S(1)}, u32[]{:S(2)}, u32[]{:S(2)}) collective-permute-start(bf16[272,512]{1,0:T(8,128)(2,1)S(1)} %concatenate.49), channel_id=1, source_target_pairs={{0,8},{1,25},{2,10},{3,27},{4,12},{5,29},{6,14},{7,31},{8,16},{9,1... | collective-permute-start | bytes 835592 | tf_op jit(solution)/shard_map/ppermute | solution.py:27
  18.7 13.6 %collective-permute-start.1 = (bf16[272,512]{1,0:T(8,128)(2,1)S(1)}, bf16[272,512]{1,0:T(8,128)(2,1)S(1)}, u32[]{:S(2)}, u32[]{:S(2)}) collective-permute-start(bf16[272,512]{1,0:T(8,128)(2,1)S(1)} %concatenate.43), channel_id=1, source_target_pairs={{0,6},{1,3},{2,0},{3,5},{4,2},{5,7},{6,4},{7,1},{8,14},{9,11},{10,... | collective-permute-start | bytes 835592 | tf_op jit(solution)/shard_map/ppermute | solution.py:27
  21.4 11.0 %collective-permute-start.7 = (bf16[272,512]{1,0:T(8,128)(2,1)S(1)}, bf16[272,512]{1,0:T(8,128)(2,1)S(1)}, u32[]{:S(2)}, u32[]{:S(2)}) collective-permute-start(bf16[272,512]{1,0:T(8,128)(2,1)S(1)} %concatenate.49), channel_id=1, source_target_pairs={{0,24},{1,9},{2,26},{3,11},{4,28},{5,13},{6,30},{7,15},{8,0},{9,17... | collective-permute-start | bytes 835592 | tf_op jit(solution)/shard_map/ppermute | solution.py:27
  25.0 20.1 %collective-permute-start.2 = (bf16[272,512]{1,0:T(8,128)(2,1)S(1)}, bf16[272,512]{1,0:T(8,128)(2,1)S(1)}, u32[]{:S(2)}, u32[]{:S(2)}) collective-permute-start(bf16[272,512]{1,0:T(8,128)(2,1)S(1)} %collective-permute-done), channel_id=1, source_target_pairs={{0,2},{1,7},{2,4},{3,1},{4,6},{5,3},{6,0},{7,5},{8,10},{9,15},{10,... | collective-permute-start | bytes 835592 | tf_op jit(solution)/shard_map/ppermute | solution.py:27
  30.3 9.7 %collective-permute-start.8 = (bf16[272,512]{1,0:T(8,128)(2,1)S(1)}, bf16[272,512]{1,0:T(8,128)(2,1)S(1)}, u32[]{:S(2)}, u32[]{:S(2)}) collective-permute-start(bf16[272,512]{1,0:T(8,128)(2,1)S(1)} %collective-permute-done.6), channel_id=1, source_target_pairs={{0,8},{1,25},{2,10},{3,27},{4,12},{5,29},{6,14},{7,31},{8,16},{9,1... | collective-permute-start | bytes 835592 | tf_op jit(solution)/shard_map/ppermute | solution.py:27
  32.3 43.3 %copy-start.1 = (s32[4]{0:T(128)S(1)}, s32[4]{0:T(128)}, u32[]{:S(2)}) copy-start(s32[4]{0:T(128)} %constant.88.clone) | copy-start | bytes 52
  40.0 28.7 %collective-permute-start.9 = (bf16[1088,512]{1,0:T(8,128)(2,1)S(1)}, bf16[1088,512]{1,0:T(8,128)(2,1)}, u32[]{:S(2)}, u32[]{:S(2)}) collective-permute-start(bf16[1088,512]{1,0:T(8,128)(2,1)S(1)} %constant_dynamic-update-slice_fusion.5.refs_4_), channel_id=1, source_target_pairs={{0,2},{1,7},{2,4},{3,1},{4,6},{5,3},{6,0},{7,5},{8,10},{9,15},{10,... | collective-permute-start | bytes 3342344 | tf_op jit(solution)/shard_map/ppermute | solution.py:27
  45.2 28.4 %collective-permute-start.3 = (bf16[1088,512]{1,0:T(8,128)(2,1)S(1)}, bf16[1088,512]{1,0:T(8,128)(2,1)}, u32[]{:S(2)}, u32[]{:S(2)}) collective-permute-start(bf16[1088,512]{1,0:T(8,128)(2,1)S(1)} %constant_dynamic-update-slice_fusion.refs_0_), channel_id=1, source_target_pairs={{0,8},{1,25},{2,10},{3,27},{4,12},{5,29},{6,14},{7,31},{8,16},{9,1... | collective-permute-start | bytes 3342344 | tf_op jit(solution)/shard_map/ppermute | solution.py:27
  47.1 28.9 %collective-permute-start.10 = (bf16[1088,512]{1,0:T(8,128)(2,1)S(1)}, bf16[1088,512]{1,0:T(8,128)(2,1)}, u32[]{:S(2)}, u32[]{:S(2)}) collective-permute-start(bf16[1088,512]{1,0:T(8,128)(2,1)S(1)} %constant_dynamic-update-slice_fusion.5.refs_4_), channel_id=1, source_target_pairs={{0,6},{1,3},{2,0},{3,5},{4,2},{5,7},{6,4},{7,1},{8,14},{9,11},{10,... | collective-permute-start | bytes 3342344 | tf_op jit(solution)/shard_map/ppermute | solution.py:27
  49.0 28.6 %collective-permute-start.4 = (bf16[1088,512]{1,0:T(8,128)(2,1)S(1)}, bf16[1088,512]{1,0:T(8,128)(2,1)}, u32[]{:S(2)}, u32[]{:S(2)}) collective-permute-start(bf16[1088,512]{1,0:T(8,128)(2,1)S(1)} %constant_dynamic-update-slice_fusion.refs_0_), channel_id=1, source_target_pairs={{0,24},{1,9},{2,26},{3,11},{4,28},{5,13},{6,30},{7,15},{8,0},{9,17... | collective-permute-start | bytes 3342344 | tf_op jit(solution)/shard_map/ppermute | solution.py:27
  68.7 17.7 %collective-permute-start.11 = (bf16[1088,512]{1,0:T(8,128)(2,1)}, bf16[1088,512]{1,0:T(8,128)(2,1)}, u32[]{:S(2)}, u32[]{:S(2)}) collective-permute-start(bf16[1088,512]{1,0:T(8,128)(2,1)} %collective-permute-done.9.refs_5_), channel_id=1, source_target_pairs={{0,2},{1,7},{2,4},{3,1},{4,6},{5,3},{6,0},{7,5},{8,10},{9,15},{10,... | collective-permute-start | bytes 3342344 | tf_op jit(solution)/shard_map/ppermute | solution.py:27
  73.6 18.6 %collective-permute-start.5 = (bf16[1088,512]{1,0:T(8,128)(2,1)}, bf16[1088,512]{1,0:T(8,128)(2,1)}, u32[]{:S(2)}, u32[]{:S(2)}) collective-permute-start(bf16[1088,512]{1,0:T(8,128)(2,1)} %collective-permute-done.3.refs_1_), channel_id=1, source_target_pairs={{0,8},{1,25},{2,10},{3,27},{4,12},{5,29},{6,14},{7,31},{8,16},{9,1... | collective-permute-start | bytes 3342344 | tf_op jit(solution)/shard_map/ppermute | solution.py:27
  109.7 21.6 %all-to-all-start = ((f32[32,1,384]{2,1,0:T(1,128)}), f32[32,1,384]{2,1,0:T(1,128)S(1)}, u32[]{:S(2)}, u32[]{:S(2)}) async-start(f32[32,1,384]{2,1,0:T(1,128)} %get-tuple-element.10), calls=%async_computation | async-start | bytes 98304 | tf_op jit(solution)/shard_map/all_to_all | solution.py:184
  117.6 13.7 %collective-permute-start.12 = (f32[256,384]{1,0:T(8,128)}, f32[256,384]{1,0:T(8,128)S(1)}, u32[]{:S(2)}, u32[]{:S(2)}) collective-permute-start(f32[256,384]{1,0:T(8,128)} %get-tuple-element.9), channel_id=1, source_target_pairs={{0,1},{1,0},{2,3},{3,2},{4,5},{5,4},{6,7},{7,6},{8,9},{9,8},{10,11... | collective-permute-start | bytes 1179656 | tf_op jit(solution)/shard_map/ppermute | solution.py:185
Sparse Core Ops, SparseCore 0:
  9.5 91.3 all-gather.2

commit v2 on v1

--- a/solution.py
+++ b/solution.py
@@ -1,3 +1,5 @@
+import functools
+
 import jax
 import jax.numpy as jnp
 from jax import lax
@@ -58,11 +60,13 @@
     sums[:SPAN] = jnp.zeros((SPAN,) + sums.shape[1:], jnp.float32)
     count = jnp.int32(0)
     for group in range(4):
-        for item in range(group * 4, group * 4 + 4):
-            fetch_piece(item, tile_refs[0], 0).wait()
-            fetch_block(item).wait()
-        for item in range(group * 4, group * 4 + 4):
-            add_product(item, item, table[0, item] // SPAN)
+        at_once = 1 if group == 0 else 4
+        for first in range(group * 4, group * 4 + 4, at_once):
+            for item in range(first, first + at_once):
+                fetch_piece(item, tile_refs[0], 0).wait()
+                fetch_block(item).wait()
+            for item in range(first, first + at_once):
+                add_product(item, item, table[0, item] // SPAN)
         for inner in range(4):
             item, mate = 16 + group * 4 + inner, inner * 4 + group
             live = table[0, item] < DEAD
@@ -77,27 +81,32 @@
                 target[count] = table[0, item] // SPAN
 
             count = count + live.astype(jnp.int32)
-    for spare in range(3):
-        order[count + spare] = 0
-        source[count + spare] = 0
-        target[count + spare] = SPAN
+    order[count] = 0
+    source[count] = 0
+    target[count] = SPAN
+    batches = (count + 1) // 4
+
+    def wait(place):
+        item = order[place]
+        fetch_piece(item, tile_refs[0], 0).wait()
+        pl.when(source[place] == item)(lambda: fetch_block(item).wait())
 
     def batch(step, carry):
         for lane in range(4):
             place = step * 4 + lane
-
-            @pl.when(place < count)
-            def _(place=place):
-                item = order[place]
-                fetch_piece(item, tile_refs[0], 0).wait()
-                pl.when(source[place] == item)(lambda: fetch_block(item).wait())
-
+            pl.when(place < count)(functools.partial(wait, place))
         for lane in range(4):
             place = step * 4 + lane
             add_product(order[place], source[place], target[place])
         return carry
 
-    lax.fori_loop(0, (count + 3) // 4, batch, 0)
+    def single(place, carry):
+        wait(place)
+        add_product(order[place], source[place], target[place])
+        return carry
+
+    lax.fori_loop(0, batches, batch, 0)
+    lax.fori_loop(batches * 4, count, single, 0)
     mine = table[2, 0]
     outs = []
     total = jnp.zeros((1, sums.shape[2]), jnp.float32)
@@ -158,7 +167,7 @@
     keep, send, mass = pl.pallas_call(
         product_kernel,
         out_shape=(
-            pltpu.HBM((rows, slab_cols), jnp.float32),
+            jax.ShapeDtypeStruct((rows, slab_cols), jnp.float32),
             pltpu.HBM((rows, slab_cols), jnp.float32),
             pltpu.HBM((members, 1, slab_cols), jnp.float32),
         ),

time: 141 us -> 140 us (level)
  the two profiles are of different devices: /device:TPU:18 before, /device:TPU:1 now
where the time goes in v2:
time: 140 us; the launch traced here: 139 us
  starting transfers between devices  53.3 us (38%)
  waiting for transfers between devices  50.1 us (36%)
  between operations  14.4 us (10%)
  local copies, waits for them, and re-layouts  11.5 us (8%)
  Pallas kernels  8.64 us (6%)
    ppermute x12, starting transfers between devices, shift(): lax.ppermute(value, ('col', 'layer'), torus_pairs((sign * step[0], sign *...  43.4 us
    ppermute x12, waiting for transfers between devices, shift(): lax.ppermute(value, ('col', 'layer'), torus_pairs((sign * step[0], sign *...  23.2 us
    all_gather x1, waiting for transfers between devices, local(): slab = lax.all_gather(slab_half, ('row', 'layer'), axis=0, tiled=True)  16.5 us
    all_to_all x1, waiting for transfers between devices, local(): parts = lax.all_to_all(mass, ('row', 'layer'), 0, 0, tiled=True)  10.4 us
    pallas_call x1, Pallas kernels, local(): pl.pallas_call(product_kernel, out_shape=(jax.ShapeDtypeStruct((rows, sla...  8.64 us
    all_to_all x1, starting transfers between devices, local(): parts = lax.all_to_all(mass, ('row', 'layer'), 0, 0, tiled=True)  7.74 us
    unnamed x20, local copies, waits for them, and re-layouts  4.39 us
    slice x8, local copies, waits for them, and re-layouts, local(): t.reshape(4, stride, tile_size)[:, rows, 0]  4.23 us
  transfers between devices with their start and end apart: 15, of which 8 were waited for; matrix products, arithmetic and copies ran while one was open for 7% of the time, Pallas kernels for 0%

profile of v2, /device:TPU:1, one launch (start us, length us, event | category | flops | bytes accessed | tf_op | source)
XLA Modules:
  0.0 139.1 jit_solution(10082131458264169462)
XLA Ops:
  6.5 1.1 copy-done
  7.7 0.8 constant_dynamic-slice_fusion
  9.1 0.6 fusion.6
  9.7 1.1 constant_dynamic-update-slice_fusion.9
  10.8 0.7 concatenate.43
  11.5 5.5 %collective-permute-start = (bf16[272,512]{1,0:T(8,128)(2,1)S(1)}, bf16[272,512]{1,0:T(8,128)(2,1)S(1)}, u32[]{:S(2)}, u32[]{:S(2)}) collective-permute-start(bf16[272,512]{1,0:T(8,128)(2,1)S(1)} %concatenate.43), channel_id=1, source_target_pairs={{0,2},{1,7},{2,4},{3,1},{4,6},{5,3},{6,0},{7,5},{8,10},{9,15},{10,... | collective-permute-start | bytes 835592 | tf_op jit(solution)/shard_map/ppermute | solution.py:29
  17.0 0.6 concatenate.49
  17.6 4.4 %collective-permute-start.6 = (bf16[272,512]{1,0:T(8,128)(2,1)S(1)}, bf16[272,512]{1,0:T(8,128)(2,1)S(1)}, u32[]{:S(2)}, u32[]{:S(2)}) collective-permute-start(bf16[272,512]{1,0:T(8,128)(2,1)S(1)} %concatenate.49), channel_id=1, source_target_pairs={{0,8},{1,25},{2,10},{3,27},{4,12},{5,29},{6,14},{7,31},{8,16},{9,1... | collective-permute-start | bytes 835592 | tf_op jit(solution)/shard_map/ppermute | solution.py:29
  22.0 1.9 %collective-permute-start.1 = (bf16[272,512]{1,0:T(8,128)(2,1)S(1)}, bf16[272,512]{1,0:T(8,128)(2,1)S(1)}, u32[]{:S(2)}, u32[]{:S(2)}) collective-permute-start(bf16[272,512]{1,0:T(8,128)(2,1)S(1)} %concatenate.43), channel_id=1, source_target_pairs={{0,6},{1,3},{2,0},{3,5},{4,2},{5,7},{6,4},{7,1},{8,14},{9,11},{10,... | collective-permute-start | bytes 835592 | tf_op jit(solution)/shard_map/ppermute | solution.py:29
  23.9 1.9 %collective-permute-start.7 = (bf16[272,512]{1,0:T(8,128)(2,1)S(1)}, bf16[272,512]{1,0:T(8,128)(2,1)S(1)}, u32[]{:S(2)}, u32[]{:S(2)}) collective-permute-start(bf16[272,512]{1,0:T(8,128)(2,1)S(1)} %concatenate.49), channel_id=1, source_target_pairs={{0,24},{1,9},{2,26},{3,11},{4,28},{5,13},{6,30},{7,15},{8,0},{9,17... | collective-permute-start | bytes 835592 | tf_op jit(solution)/shard_map/ppermute | solution.py:29
  25.8 1.2 constant_dynamic-update-slice_fusion.3
  27.0 4.6 %collective-permute-start.2 = (bf16[272,512]{1,0:T(8,128)(2,1)S(1)}, bf16[272,512]{1,0:T(8,128)(2,1)S(1)}, u32[]{:S(2)}, u32[]{:S(2)}) collective-permute-start(bf16[272,512]{1,0:T(8,128)(2,1)S(1)} %collective-permute-done), channel_id=1, source_target_pairs={{0,2},{1,7},{2,4},{3,1},{4,6},{5,3},{6,0},{7,5},{8,10},{9,15},{10,... | collective-permute-start | bytes 835592 | tf_op jit(solution)/shard_map/ppermute | solution.py:29
  31.6 4.6 %collective-permute-start.8 = (bf16[272,512]{1,0:T(8,128)(2,1)S(1)}, bf16[272,512]{1,0:T(8,128)(2,1)S(1)}, u32[]{:S(2)}, u32[]{:S(2)}) collective-permute-start(bf16[272,512]{1,0:T(8,128)(2,1)S(1)} %collective-permute-done.6), channel_id=1, source_target_pairs={{0,8},{1,25},{2,10},{3,27},{4,12},{5,29},{6,14},{7,31},{8,16},{9,1... | collective-permute-start | bytes 835592 | tf_op jit(solution)/shard_map/ppermute | solution.py:29
  36.3 3.4 %collective-permute-done.8 = bf16[272,512]{1,0:T(8,128)(2,1)S(1)} collective-permute-done((bf16[272,512]{1,0:T(8,128)(2,1)S(1)}, bf16[272,512]{1,0:T(8,128)(2,1)S(1)}, u32[]{:S(2)}, u32[]{:S(2)}) %collective-permute-start.8) | collective-permute-done | bytes 278560 | tf_op jit(solution)/shard_map/ppermute | solution.py:29
  39.7 1.9 %collective-permute-start.9 = (bf16[1088,512]{1,0:T(8,128)(2,1)S(1)}, bf16[1088,512]{1,0:T(8,128)(2,1)}, u32[]{:S(2)}, u32[]{:S(2)}) collective-permute-start(bf16[1088,512]{1,0:T(8,128)(2,1)S(1)} %constant_dynamic-update-slice_fusion.5.refs_4_), channel_id=1, source_target_pairs={{0,2},{1,7},{2,4},{3,1},{4,6},{5,3},{6,0},{7,5},{8,10},{9,15},{10,... | collective-permute-start | bytes 3342344 | tf_op jit(solution)/shard_map/ppermute | solution.py:29
  41.7 5.4 %collective-permute-start.3 = (bf16[1088,512]{1,0:T(8,128)(2,1)S(1)}, bf16[1088,512]{1,0:T(8,128)(2,1)}, u32[]{:S(2)}, u32[]{:S(2)}) collective-permute-start(bf16[1088,512]{1,0:T(8,128)(2,1)S(1)} %constant_dynamic-update-slice_fusion.refs_0_), channel_id=1, source_target_pairs={{0,8},{1,25},{2,10},{3,27},{4,12},{5,29},{6,14},{7,31},{8,16},{9,1... | collective-permute-start | bytes 3342344 | tf_op jit(solution)/shard_map/ppermute | solution.py:29
  47.1 3.4 %collective-permute-start.10 = (bf16[1088,512]{1,0:T(8,128)(2,1)S(1)}, bf16[1088,512]{1,0:T(8,128)(2,1)}, u32[]{:S(2)}, u32[]{:S(2)}) collective-permute-start(bf16[1088,512]{1,0:T(8,128)(2,1)S(1)} %constant_dynamic-update-slice_fusion.5.refs_4_), channel_id=1, source_target_pairs={{0,6},{1,3},{2,0},{3,5},{4,2},{5,7},{6,4},{7,1},{8,14},{9,11},{10,... | collective-permute-start | bytes 3342344 | tf_op jit(solution)/shard_map/ppermute | solution.py:29
  50.5 1.9 %collective-permute-start.4 = (bf16[1088,512]{1,0:T(8,128)(2,1)S(1)}, bf16[1088,512]{1,0:T(8,128)(2,1)}, u32[]{:S(2)}, u32[]{:S(2)}) collective-permute-start(bf16[1088,512]{1,0:T(8,128)(2,1)S(1)} %constant_dynamic-update-slice_fusion.refs_0_), channel_id=1, source_target_pairs={{0,24},{1,9},{2,26},{3,11},{4,28},{5,13},{6,30},{7,15},{8,0},{9,17... | collective-permute-start | bytes 3342344 | tf_op jit(solution)/shard_map/ppermute | solution.py:29
  52.4 5.3 %collective-permute-done.9.refs_5_ = bf16[1088,512]{1,0:T(8,128)(2,1)} collective-permute-done((bf16[1088,512]{1,0:T(8,128)(2,1)S(1)}, bf16[1088,512]{1,0:T(8,128)(2,1)}, u32[]{:S(2)}, u32[]{:S(2)}) %collective-permute-start.9) | collective-permute-done | bytes 1114144 | tf_op jit(solution)/shard_map/ppermute | solution.py:29
  57.7 1.9 %collective-permute-start.11 = (bf16[1088,512]{1,0:T(8,128)(2,1)}, bf16[1088,512]{1,0:T(8,128)(2,1)}, u32[]{:S(2)}, u32[]{:S(2)}) collective-permute-start(bf16[1088,512]{1,0:T(8,128)(2,1)} %collective-permute-done.9.refs_5_), channel_id=1, source_target_pairs={{0,2},{1,7},{2,4},{3,1},{4,6},{5,3},{6,0},{7,5},{8,10},{9,15},{10,... | collective-permute-start | bytes 3342344 | tf_op jit(solution)/shard_map/ppermute | solution.py:29
  59.7 6.0 %collective-permute-start.5 = (bf16[1088,512]{1,0:T(8,128)(2,1)}, bf16[1088,512]{1,0:T(8,128)(2,1)}, u32[]{:S(2)}, u32[]{:S(2)}) collective-permute-start(bf16[1088,512]{1,0:T(8,128)(2,1)} %collective-permute-done.3.refs_1_), channel_id=1, source_target_pairs={{0,8},{1,25},{2,10},{3,27},{4,12},{5,29},{6,14},{7,31},{8,16},{9,1... | collective-permute-start | bytes 3342344 | tf_op jit(solution)/shard_map/ppermute | solution.py:29
  65.7 0.1 pad.6.clone
  65.9 0.1 sub.27
  66.0 0.1 copy.14
  66.1 0.1 copy.18
  66.2 10.0 %collective-permute-done.10.refs_6_ = bf16[1088,512]{1,0:T(8,128)(2,1)} collective-permute-done((bf16[1088,512]{1,0:T(8,128)(2,1)S(1)}, bf16[1088,512]{1,0:T(8,128)(2,1)}, u32[]{:S(2)}, u32[]{:S(2)}) %collective-permute-start.10) | collective-permute-done | bytes 1114144 | tf_op jit(solution)/shard_map/ppermute | solution.py:29
  76.2 0.7 slice.46
  76.9 0.1 copy.20
  77.0 0.7 slice.45
  77.7 0.1 copy.19
  77.8 0.3 collective-permute-done.4.refs_2_
  78.1 0.7 slice.42
  78.8 0.1 copy.16
  79.0 0.7 slice.41
  79.7 0.1 copy.15
  79.8 0.5 collective-permute-done.11.refs_7_
  80.2 0.7 slice.47
  81.0 0.1 copy.21
  81.1 3.7 %collective-permute-done.5.refs_3_ = bf16[1088,512]{1,0:T(8,128)(2,1)} collective-permute-done((bf16[1088,512]{1,0:T(8,128)(2,1)}, bf16[1088,512]{1,0:T(8,128)(2,1)}, u32[]{:S(2)}, u32[]{:S(2)}) %collective-permute-start.5) | collective-permute-done | bytes 1114144 | tf_op jit(solution)/shard_map/ppermute | solution.py:29
  84.7 0.7 slice.43
  85.5 0.1 copy.17
  85.6 0.1 concatenate.55
  85.7 16.5 %all-gather.3.cloned.1.call-done = bf16[1,1,16384,384]{3,2,1,0:T(8,128)(2,1)} async-done(((bf16[1,1,512,384]{3,2,1,0:T(8,128)(2,1)}), bf16[1,1,16384,384]{3,2,1,0:T(8,128)(2,1)}) %all-gather.3.cloned.1.call-update) | async-done | bytes 12582928 | tf_op jit(solution)/shard_map/all_gather | solution.py:138
  102.3 8.6 %shard_map.55 = (f32[256,384]{1,0:T(8,128)S(1)}, f32[256,384]{1,0:T(8,128)}, f32[32,1,384]{2,1,0:T(1,128)}) custom-call(s32[3,32]{1,0:T(4,128)S(1)} %add_add_fusion.1.table, bf16[1088,512]{1,0:T(8,128)(2,1)S(1)} %constant_dynamic-update-slice_fusion.refs_0_, bf16[1088,512]{1,0:T(8,128)(2,1)} %collective-permute-done.3.refs_1_, ...), custom_call_target="tpu_custom_call" | custom-call | flops 3221225472 | bytes 20971520 | tf_op jit(solution)/shard_map/pallas_call | solution.py:167
  110.9 7.7 %all-to-all-start = ((f32[32,1,384]{2,1,0:T(1,128)}), f32[32,1,384]{2,1,0:T(1,128)S(1)}, u32[]{:S(2)}, u32[]{:S(2)}) async-start(f32[32,1,384]{2,1,0:T(1,128)} %get-tuple-element.10), calls=%async_computation | async-start | bytes 98304 | tf_op jit(solution)/shard_map/all_to_all | solution.py:193
  118.7 2.1 %collective-permute-start.12 = (f32[256,384]{1,0:T(8,128)}, f32[256,384]{1,0:T(8,128)S(1)}, u32[]{:S(2)}, u32[]{:S(2)}) collective-permute-start(f32[256,384]{1,0:T(8,128)} %get-tuple-element.9), channel_id=1, source_target_pairs={{0,1},{1,0},{2,3},{3,2},{4,5},{5,4},{6,7},{7,6},{8,9},{9,8},{10,11... | collective-permute-start | bytes 1179656 | tf_op jit(solution)/shard_map/ppermute | solution.py:194
  120.8 10.4 %all-to-all-done = f32[32,1,384]{2,1,0:T(1,128)S(1)} async-done(((f32[32,1,384]{2,1,0:T(1,128)}), f32[32,1,384]{2,1,0:T(1,128)S(1)}, u32[]{:S(2)}, u32[]{:S(2)}) %all-to-all-start) | async-done | bytes 49184 | tf_op jit(solution)/shard_map/all_to_all | solution.py:193
  131.3 0.9 maximum_divide_fusion
  (32 shorter events, 0.5 us)
Async XLA Ops:
  6.5 1.1 copy-start
  6.5 2.6 %copy-start.2 = (s32[1,1,2]{2,1,0:T(1,128)S(1)}, s32[1,1,2]{2,1,0:T(1,128)}, u32[]{:S(2)}) copy-start(s32[1,1,2]{2,1,0:T(1,128)} %param.6) | copy-start | bytes 28
  6.5 95.7 %all-gather.3.cloned.1.call-start = ((), (), s32[]{:S(2)}) async-start(), calls=%async_computation.1 | async-start | bytes 12976128 | tf_op jit(solution)/shard_map/all_gather | solution.py:138
  11.5 15.5 %collective-permute-start = (bf16[272,512]{1,0:T(8,128)(2,1)S(1)}, bf16[272,512]{1,0:T(8,128)(2,1)S(1)}, u32[]{:S(2)}, u32[]{:S(2)}) collective-permute-start(bf16[272,512]{1,0:T(8,128)(2,1)S(1)} %concatenate.43), channel_id=1, source_target_pairs={{0,2},{1,7},{2,4},{3,1},{4,6},{5,3},{6,0},{7,5},{8,10},{9,15},{10,... | collective-permute-start | bytes 835592 | tf_op jit(solution)/shard_map/ppermute | solution.py:29
  17.6 14.1 %collective-permute-start.6 = (bf16[272,512]{1,0:T(8,128)(2,1)S(1)}, bf16[272,512]{1,0:T(8,128)(2,1)S(1)}, u32[]{:S(2)}, u32[]{:S(2)}) collective-permute-start(bf16[272,512]{1,0:T(8,128)(2,1)S(1)} %concatenate.49), channel_id=1, source_target_pairs={{0,8},{1,25},{2,10},{3,27},{4,12},{5,29},{6,14},{7,31},{8,16},{9,1... | collective-permute-start | bytes 835592 | tf_op jit(solution)/shard_map/ppermute | solution.py:29
  22.0 14.3 %collective-permute-start.1 = (bf16[272,512]{1,0:T(8,128)(2,1)S(1)}, bf16[272,512]{1,0:T(8,128)(2,1)S(1)}, u32[]{:S(2)}, u32[]{:S(2)}) collective-permute-start(bf16[272,512]{1,0:T(8,128)(2,1)S(1)} %concatenate.43), channel_id=1, source_target_pairs={{0,6},{1,3},{2,0},{3,5},{4,2},{5,7},{6,4},{7,1},{8,14},{9,11},{10,... | collective-permute-start | bytes 835592 | tf_op jit(solution)/shard_map/ppermute | solution.py:29
  23.9 12.4 %collective-permute-start.7 = (bf16[272,512]{1,0:T(8,128)(2,1)S(1)}, bf16[272,512]{1,0:T(8,128)(2,1)S(1)}, u32[]{:S(2)}, u32[]{:S(2)}) collective-permute-start(bf16[272,512]{1,0:T(8,128)(2,1)S(1)} %concatenate.49), channel_id=1, source_target_pairs={{0,24},{1,9},{2,26},{3,11},{4,28},{5,13},{6,30},{7,15},{8,0},{9,17... | collective-permute-start | bytes 835592 | tf_op jit(solution)/shard_map/ppermute | solution.py:29
  27.0 14.6 %collective-permute-start.2 = (bf16[272,512]{1,0:T(8,128)(2,1)S(1)}, bf16[272,512]{1,0:T(8,128)(2,1)S(1)}, u32[]{:S(2)}, u32[]{:S(2)}) collective-permute-start(bf16[272,512]{1,0:T(8,128)(2,1)S(1)} %collective-permute-done), channel_id=1, source_target_pairs={{0,2},{1,7},{2,4},{3,1},{4,6},{5,3},{6,0},{7,5},{8,10},{9,15},{10,... | collective-permute-start | bytes 835592 | tf_op jit(solution)/shard_map/ppermute | solution.py:29
  31.6 8.1 %collective-permute-start.8 = (bf16[272,512]{1,0:T(8,128)(2,1)S(1)}, bf16[272,512]{1,0:T(8,128)(2,1)S(1)}, u32[]{:S(2)}, u32[]{:S(2)}) collective-permute-start(bf16[272,512]{1,0:T(8,128)(2,1)S(1)} %collective-permute-done.6), channel_id=1, source_target_pairs={{0,8},{1,25},{2,10},{3,27},{4,12},{5,29},{6,14},{7,31},{8,16},{9,1... | collective-permute-start | bytes 835592 | tf_op jit(solution)/shard_map/ppermute | solution.py:29
  36.3 29.5 %copy-start.1 = (s32[4]{0:T(128)S(1)}, s32[4]{0:T(128)}, u32[]{:S(2)}) copy-start(s32[4]{0:T(128)} %constant.88.clone) | copy-start | bytes 52
  39.7 18.0 %collective-permute-start.9 = (bf16[1088,512]{1,0:T(8,128)(2,1)S(1)}, bf16[1088,512]{1,0:T(8,128)(2,1)}, u32[]{:S(2)}, u32[]{:S(2)}) collective-permute-start(bf16[1088,512]{1,0:T(8,128)(2,1)S(1)} %constant_dynamic-update-slice_fusion.5.refs_4_), channel_id=1, source_target_pairs={{0,2},{1,7},{2,4},{3,1},{4,6},{5,3},{6,0},{7,5},{8,10},{9,15},{10,... | collective-permute-start | bytes 3342344 | tf_op jit(solution)/shard_map/ppermute | solution.py:29
  41.7 18.0 %collective-permute-start.3 = (bf16[1088,512]{1,0:T(8,128)(2,1)S(1)}, bf16[1088,512]{1,0:T(8,128)(2,1)}, u32[]{:S(2)}, u32[]{:S(2)}) collective-permute-start(bf16[1088,512]{1,0:T(8,128)(2,1)S(1)} %constant_dynamic-update-slice_fusion.refs_0_), channel_id=1, source_target_pairs={{0,8},{1,25},{2,10},{3,27},{4,12},{5,29},{6,14},{7,31},{8,16},{9,1... | collective-permute-start | bytes 3342344 | tf_op jit(solution)/shard_map/ppermute | solution.py:29
  47.1 29.1 %collective-permute-start.10 = (bf16[1088,512]{1,0:T(8,128)(2,1)S(1)}, bf16[1088,512]{1,0:T(8,128)(2,1)}, u32[]{:S(2)}, u32[]{:S(2)}) collective-permute-start(bf16[1088,512]{1,0:T(8,128)(2,1)S(1)} %constant_dynamic-update-slice_fusion.5.refs_4_), channel_id=1, source_target_pairs={{0,6},{1,3},{2,0},{3,5},{4,2},{5,7},{6,4},{7,1},{8,14},{9,11},{10,... | collective-permute-start | bytes 3342344 | tf_op jit(solution)/shard_map/ppermute | solution.py:29
  50.5 27.6 %collective-permute-start.4 = (bf16[1088,512]{1,0:T(8,128)(2,1)S(1)}, bf16[1088,512]{1,0:T(8,128)(2,1)}, u32[]{:S(2)}, u32[]{:S(2)}) collective-permute-start(bf16[1088,512]{1,0:T(8,128)(2,1)S(1)} %constant_dynamic-update-slice_fusion.refs_0_), channel_id=1, source_target_pairs={{0,24},{1,9},{2,26},{3,11},{4,28},{5,13},{6,30},{7,15},{8,0},{9,17... | collective-permute-start | bytes 3342344 | tf_op jit(solution)/shard_map/ppermute | solution.py:29
  57.7 22.5 %collective-permute-start.11 = (bf16[1088,512]{1,0:T(8,128)(2,1)}, bf16[1088,512]{1,0:T(8,128)(2,1)}, u32[]{:S(2)}, u32[]{:S(2)}) collective-permute-start(bf16[1088,512]{1,0:T(8,128)(2,1)} %collective-permute-done.9.refs_5_), channel_id=1, source_target_pairs={{0,2},{1,7},{2,4},{3,1},{4,6},{5,3},{6,0},{7,5},{8,10},{9,15},{10,... | collective-permute-start | bytes 3342344 | tf_op jit(solution)/shard_map/ppermute | solution.py:29
  59.7 25.1 %collective-permute-start.5 = (bf16[1088,512]{1,0:T(8,128)(2,1)}, bf16[1088,512]{1,0:T(8,128)(2,1)}, u32[]{:S(2)}, u32[]{:S(2)}) collective-permute-start(bf16[1088,512]{1,0:T(8,128)(2,1)} %collective-permute-done.3.refs_1_), channel_id=1, source_target_pairs={{0,8},{1,25},{2,10},{3,27},{4,12},{5,29},{6,14},{7,31},{8,16},{9,1... | collective-permute-start | bytes 3342344 | tf_op jit(solution)/shard_map/ppermute | solution.py:29
  110.9 20.3 %all-to-all-start = ((f32[32,1,384]{2,1,0:T(1,128)}), f32[32,1,384]{2,1,0:T(1,128)S(1)}, u32[]{:S(2)}, u32[]{:S(2)}) async-start(f32[32,1,384]{2,1,0:T(1,128)} %get-tuple-element.10), calls=%async_computation | async-start | bytes 98304 | tf_op jit(solution)/shard_map/all_to_all | solution.py:193
  118.7 12.6 %collective-permute-start.12 = (f32[256,384]{1,0:T(8,128)}, f32[256,384]{1,0:T(8,128)S(1)}, u32[]{:S(2)}, u32[]{:S(2)}) collective-permute-start(f32[256,384]{1,0:T(8,128)} %get-tuple-element.9), channel_id=1, source_target_pairs={{0,1},{1,0},{2,3},{3,2},{4,5},{5,4},{6,7},{7,6},{8,9},{9,8},{10,11... | collective-permute-start | bytes 1179656 | tf_op jit(solution)/shard_map/ppermute | solution.py:194
Sparse Core Ops, SparseCore 0:
  9.5 92.7 all-gather.2

commit v3 on v2

--- a/solution.py
+++ b/solution.py
@@ -121,6 +121,19 @@
     outs.append(pltpu.make_async_copy(spread, mass, out_sem.at[2]))
     outs[-1].start()
     for copy in outs:
+        copy.wait()
+
+
+def finish_kernel(matrix_order, layer, parts, keep, other, out, halves, sems):
+    rows = keep.shape[0]
+    scale = jnp.sum(parts[...], axis=0) / matrix_order + 1e-06
+    copies = []
+    for at, (value, half) in enumerate(((keep, layer[0]), (other, 1 - layer[0]))):
+        halves[at] = value[...] / scale
+        first = pl.multiple_of(half * rows, rows)
+        copies.append(pltpu.make_async_copy(halves.at[at], out.at[pl.ds(first, rows), :], sems.at[at]))
+        copies[-1].start()
+    for copy in copies:
         copy.wait()
 
 
@@ -192,10 +205,17 @@
     matrix_order = grid_size * SPAN * tile_size
     parts = lax.all_to_all(mass, ("row", "layer"), 0, 0, tiled=True)
     other = lax.ppermute(send, "layer", [(0, 1), (1, 0)])
-    lower = layer == 0
-    halves = jnp.where(lower, keep, other), jnp.where(lower, other, keep)
-    column_mass = jnp.sum(parts, axis=(0, 1)) / matrix_order
-    return jnp.concatenate(halves, 0) / (column_mass + 1e-06)
+    return pl.pallas_call(
+        functools.partial(finish_kernel, matrix_order),
+        out_shape=jax.ShapeDtypeStruct((tile_size, slab_cols), jnp.float32),
+        in_specs=[pl.BlockSpec(memory_space=pltpu.SMEM)] + [pl.BlockSpec(memory_space=pltpu.VMEM)] * 3,
+        out_specs=pl.BlockSpec(memory_space=pl.ANY),
+        scratch_shapes=[
+            pltpu.VMEM((SPAN, rows, slab_cols), jnp.float32),
+            pltpu.SemaphoreType.DMA((SPAN,)),
+        ],
+        compiler_params=pltpu.CompilerParams(vmem_limit_bytes=8 << 20),
+    )(layer[None], parts, keep, other)
 
 
 def solution(mesh):

time: 140 us -> 142 us (1.014)
  the two profiles are of different devices: /device:TPU:1 before, /device:TPU:16 now
where the time goes in v3:
time: 142 us; the launch traced here: 141 us
  starting transfers between devices  44 us (31%)
  waiting for transfers between devices  39.8 us (28%)
  blocking collectives  21.9 us (15%)
  between operations  14.4 us (10%)
  local copies, waits for them, and re-layouts  11.5 us (8%)
  Pallas kernels  9.42 us (7%)
    ppermute x12, starting transfers between devices, shift(): lax.ppermute(value, ('col', 'layer'), torus_pairs((sign * step[0], sign *...  41.9 us
    ppermute x12, waiting for transfers between devices, shift(): lax.ppermute(value, ('col', 'layer'), torus_pairs((sign * step[0], sign *...  34.8 us
    all_to_all x1, blocking collectives, local(): parts = lax.all_to_all(mass, ('row', 'layer'), 0, 0, tiled=True)  21.9 us
    pallas_call x1, Pallas kernels, local(): pl.pallas_call(product_kernel, out_shape=(jax.ShapeDtypeStruct((rows, sla...  8.45 us
    all_gather x1, waiting for transfers between devices, local(): slab = lax.all_gather(slab_half, ('row', 'layer'), axis=0, tiled=True)  4.93 us
    unnamed x20, local copies, waits for them, and re-layouts  4.37 us
    slice x8, local copies, waits for them, and re-layouts, local(): t.reshape(4, stride, tile_size)[:, rows, 0]  4.24 us
  transfers between devices with their start and end apart: 14, of which 6 were waited for; matrix products, arithmetic and copies ran while one was open for 7% of the time, Pallas kernels for 0%

profile of v3, /device:TPU:16, one launch (start us, length us, event | category | flops | bytes accessed | tf_op | source)
XLA Modules:
  0.0 141.2 jit_solution(911289900671168911)
XLA Ops:
  6.5 1.1 copy-done
  7.7 0.8 constant_dynamic-slice_fusion
  9.1 0.6 fusion.6
  9.8 1.1 constant_dynamic-update-slice_fusion.9
  10.9 0.6 concatenate.40
  11.5 3.2 %collective-permute-start = (bf16[272,512]{1,0:T(8,128)(2,1)S(1)}, bf16[272,512]{1,0:T(8,128)(2,1)S(1)}, u32[]{:S(2)}, u32[]{:S(2)}) collective-permute-start(bf16[272,512]{1,0:T(8,128)(2,1)S(1)} %concatenate.40), channel_id=1, source_target_pairs={{0,2},{1,7},{2,4},{3,1},{4,6},{5,3},{6,0},{7,5},{8,10},{9,15},{10,... | collective-permute-start | bytes 835592 | tf_op jit(solution)/shard_map/ppermute | solution.py:29
  14.7 0.6 concatenate.46
  15.3 3.4 %collective-permute-start.6 = (bf16[272,512]{1,0:T(8,128)(2,1)S(1)}, bf16[272,512]{1,0:T(8,128)(2,1)S(1)}, u32[]{:S(2)}, u32[]{:S(2)}) collective-permute-start(bf16[272,512]{1,0:T(8,128)(2,1)S(1)} %concatenate.46), channel_id=1, source_target_pairs={{0,8},{1,25},{2,10},{3,27},{4,12},{5,29},{6,14},{7,31},{8,16},{9,1... | collective-permute-start | bytes 835592 | tf_op jit(solution)/shard_map/ppermute | solution.py:29
  18.7 2.7 %collective-permute-start.1 = (bf16[272,512]{1,0:T(8,128)(2,1)S(1)}, bf16[272,512]{1,0:T(8,128)(2,1)S(1)}, u32[]{:S(2)}, u32[]{:S(2)}) collective-permute-start(bf16[272,512]{1,0:T(8,128)(2,1)S(1)} %concatenate.40), channel_id=1, source_target_pairs={{0,6},{1,3},{2,0},{3,5},{4,2},{5,7},{6,4},{7,1},{8,14},{9,11},{10,... | collective-permute-start | bytes 835592 | tf_op jit(solution)/shard_map/ppermute | solution.py:29
  21.4 3.7 %collective-permute-start.7 = (bf16[272,512]{1,0:T(8,128)(2,1)S(1)}, bf16[272,512]{1,0:T(8,128)(2,1)S(1)}, u32[]{:S(2)}, u32[]{:S(2)}) collective-permute-start(bf16[272,512]{1,0:T(8,128)(2,1)S(1)} %concatenate.46), channel_id=1, source_target_pairs={{0,24},{1,9},{2,26},{3,11},{4,28},{5,13},{6,30},{7,15},{8,0},{9,17... | collective-permute-start | bytes 835592 | tf_op jit(solution)/shard_map/ppermute | solution.py:29
  25.0 1.2 constant_dynamic-update-slice_fusion.3
  26.2 6.7 %collective-permute-start.2 = (bf16[272,512]{1,0:T(8,128)(2,1)S(1)}, bf16[272,512]{1,0:T(8,128)(2,1)S(1)}, u32[]{:S(2)}, u32[]{:S(2)}) collective-permute-start(bf16[272,512]{1,0:T(8,128)(2,1)S(1)} %collective-permute-done), channel_id=1, source_target_pairs={{0,2},{1,7},{2,4},{3,1},{4,6},{5,3},{6,0},{7,5},{8,10},{9,15},{10,... | collective-permute-start | bytes 835592 | tf_op jit(solution)/shard_map/ppermute | solution.py:29
  33.0 1.9 %collective-permute-start.8 = (bf16[272,512]{1,0:T(8,128)(2,1)S(1)}, bf16[272,512]{1,0:T(8,128)(2,1)S(1)}, u32[]{:S(2)}, u32[]{:S(2)}) collective-permute-start(bf16[272,512]{1,0:T(8,128)(2,1)S(1)} %collective-permute-done.6), channel_id=1, source_target_pairs={{0,8},{1,25},{2,10},{3,27},{4,12},{5,29},{6,14},{7,31},{8,16},{9,1... | collective-permute-start | bytes 835592 | tf_op jit(solution)/shard_map/ppermute | solution.py:29
  35.1 7.6 %collective-permute-done.8 = bf16[272,512]{1,0:T(8,128)(2,1)S(1)} collective-permute-done((bf16[272,512]{1,0:T(8,128)(2,1)S(1)}, bf16[272,512]{1,0:T(8,128)(2,1)S(1)}, u32[]{:S(2)}, u32[]{:S(2)}) %collective-permute-start.8) | collective-permute-done | bytes 278560 | tf_op jit(solution)/shard_map/ppermute | solution.py:29
  42.7 5.1 %collective-permute-start.9 = (bf16[1088,512]{1,0:T(8,128)(2,1)S(1)}, bf16[1088,512]{1,0:T(8,128)(2,1)}, u32[]{:S(2)}, u32[]{:S(2)}) collective-permute-start(bf16[1088,512]{1,0:T(8,128)(2,1)S(1)} %constant_dynamic-update-slice_fusion.5.refs_4_), channel_id=1, source_target_pairs={{0,2},{1,7},{2,4},{3,1},{4,6},{5,3},{6,0},{7,5},{8,10},{9,15},{10,... | collective-permute-start | bytes 3342344 | tf_op jit(solution)/shard_map/ppermute | solution.py:29
  47.9 1.9 %collective-permute-start.3 = (bf16[1088,512]{1,0:T(8,128)(2,1)S(1)}, bf16[1088,512]{1,0:T(8,128)(2,1)}, u32[]{:S(2)}, u32[]{:S(2)}) collective-permute-start(bf16[1088,512]{1,0:T(8,128)(2,1)S(1)} %constant_dynamic-update-slice_fusion.refs_0_), channel_id=1, source_target_pairs={{0,8},{1,25},{2,10},{3,27},{4,12},{5,29},{6,14},{7,31},{8,16},{9,1... | collective-permute-start | bytes 3342344 | tf_op jit(solution)/shard_map/ppermute | solution.py:29
  49.8 1.9 %collective-permute-start.10 = (bf16[1088,512]{1,0:T(8,128)(2,1)S(1)}, bf16[1088,512]{1,0:T(8,128)(2,1)}, u32[]{:S(2)}, u32[]{:S(2)}) collective-permute-start(bf16[1088,512]{1,0:T(8,128)(2,1)S(1)} %constant_dynamic-update-slice_fusion.5.refs_4_), channel_id=1, source_target_pairs={{0,6},{1,3},{2,0},{3,5},{4,2},{5,7},{6,4},{7,1},{8,14},{9,11},{10,... | collective-permute-start | bytes 3342344 | tf_op jit(solution)/shard_map/ppermute | solution.py:29
  51.7 5.1 %collective-permute-start.4 = (bf16[1088,512]{1,0:T(8,128)(2,1)S(1)}, bf16[1088,512]{1,0:T(8,128)(2,1)}, u32[]{:S(2)}, u32[]{:S(2)}) collective-permute-start(bf16[1088,512]{1,0:T(8,128)(2,1)S(1)} %constant_dynamic-update-slice_fusion.refs_0_), channel_id=1, source_target_pairs={{0,24},{1,9},{2,26},{3,11},{4,28},{5,13},{6,30},{7,15},{8,0},{9,17... | collective-permute-start | bytes 3342344 | tf_op jit(solution)/shard_map/ppermute | solution.py:29
  56.9 13.9 %collective-permute-done.9.refs_5_ = bf16[1088,512]{1,0:T(8,128)(2,1)} collective-permute-done((bf16[1088,512]{1,0:T(8,128)(2,1)S(1)}, bf16[1088,512]{1,0:T(8,128)(2,1)}, u32[]{:S(2)}, u32[]{:S(2)}) %collective-permute-start.9) | collective-permute-done | bytes 1114144 | tf_op jit(solution)/shard_map/ppermute | solution.py:29
  70.7 4.3 %collective-permute-start.11 = (bf16[1088,512]{1,0:T(8,128)(2,1)}, bf16[1088,512]{1,0:T(8,128)(2,1)}, u32[]{:S(2)}, u32[]{:S(2)}) collective-permute-start(bf16[1088,512]{1,0:T(8,128)(2,1)} %collective-permute-done.9.refs_5_), channel_id=1, source_target_pairs={{0,2},{1,7},{2,4},{3,1},{4,6},{5,3},{6,0},{7,5},{8,10},{9,15},{10,... | collective-permute-start | bytes 3342344 | tf_op jit(solution)/shard_map/ppermute | solution.py:29
  75.1 0.9 collective-permute-done.3.refs_1_
  76.0 1.9 %collective-permute-start.5 = (bf16[1088,512]{1,0:T(8,128)(2,1)}, bf16[1088,512]{1,0:T(8,128)(2,1)}, u32[]{:S(2)}, u32[]{:S(2)}) collective-permute-start(bf16[1088,512]{1,0:T(8,128)(2,1)} %collective-permute-done.3.refs_1_), channel_id=1, source_target_pairs={{0,8},{1,25},{2,10},{3,27},{4,12},{5,29},{6,14},{7,31},{8,16},{9,1... | collective-permute-start | bytes 3342344 | tf_op jit(solution)/shard_map/ppermute | solution.py:29
  77.9 0.1 pad.4.clone
  78.0 0.1 broadcast_add_fusion.1
  78.1 0.1 sub.27
  78.2 0.1 copy.14
  78.3 0.1 copy.18
  78.5 0.7 slice.46
  79.2 0.1 copy.20
  79.3 0.7 slice.45
  80.0 0.1 copy.19
  80.1 0.7 slice.42
  80.8 0.1 copy.16
  80.9 0.7 slice.41
  81.6 0.1 copy.15
  81.7 6.7 %collective-permute-done.11.refs_7_ = bf16[1088,512]{1,0:T(8,128)(2,1)} collective-permute-done((bf16[1088,512]{1,0:T(8,128)(2,1)}, bf16[1088,512]{1,0:T(8,128)(2,1)}, u32[]{:S(2)}, u32[]{:S(2)}) %collective-permute-start.11) | collective-permute-done | bytes 1114144 | tf_op jit(solution)/shard_map/ppermute | solution.py:29
  88.4 0.7 slice.47
  89.2 0.1 copy.21
  89.3 5.6 %collective-permute-done.5.refs_3_ = bf16[1088,512]{1,0:T(8,128)(2,1)} collective-permute-done((bf16[1088,512]{1,0:T(8,128)(2,1)}, bf16[1088,512]{1,0:T(8,128)(2,1)}, u32[]{:S(2)}, u32[]{:S(2)}) %collective-permute-start.5) | collective-permute-done | bytes 1114144 | tf_op jit(solution)/shard_map/ppermute | solution.py:29
  94.9 0.7 slice.43
  95.6 0.1 copy.17
  95.7 0.1 concatenate.52
  95.8 0.1 add_add_fusion.1.table
  95.9 4.9 %all-gather.3.cloned.1.call-done = bf16[1,1,16384,384]{3,2,1,0:T(8,128)(2,1)} async-done(((bf16[1,1,512,384]{3,2,1,0:T(8,128)(2,1)}), bf16[1,1,16384,384]{3,2,1,0:T(8,128)(2,1)}) %all-gather.3.cloned.1.call-update) | async-done | bytes 12582928 | tf_op jit(solution)/shard_map/all_gather | solution.py:151
  100.8 8.4 %shard_map.55 = (f32[256,384]{1,0:T(8,128)S(1)}, f32[256,384]{1,0:T(8,128)}, f32[32,1,384]{2,1,0:T(1,128)}) custom-call(s32[3,32]{1,0:T(4,128)S(1)} %add_add_fusion.1.table, bf16[1088,512]{1,0:T(8,128)(2,1)S(1)} %constant_dynamic-update-slice_fusion.refs_0_, bf16[1088,512]{1,0:T(8,128)(2,1)} %collective-permute-done.3.refs_1_, ...), custom_call_target="tpu_custom_call" | custom-call | flops 3221225472 | bytes 20971520 | tf_op jit(solution)/shard_map/pallas_call | solution.py:180
  109.3 2.1 %collective-permute-start.12 = (f32[256,384]{1,0:T(8,128)}, f32[256,384]{1,0:T(8,128)S(1)}, u32[]{:S(2)}, u32[]{:S(2)}) collective-permute-start(f32[256,384]{1,0:T(8,128)} %get-tuple-element.10), channel_id=1, source_target_pairs={{0,1},{1,0},{2,3},{3,2},{4,5},{5,4},{6,7},{7,6},{8,9},{9,8},{10,11... | collective-permute-start | bytes 1179656 | tf_op jit(solution)/shard_map/ppermute | solution.py:207
  111.4 21.9 %all_to_all.5.parts = f32[32,1,384]{2,1,0:T(1,128)S(1)} all-to-all(f32[32,1,384]{2,1,0:T(1,128)} %get-tuple-element.8), channel_id=1, replica_groups=mesh['row'=16,'col'=16,'layer'=2] {'row','layer'}, dimensions={0} | all-to-all | bytes 98304 | tf_op jit(solution)/shard_map/all_to_all | solution.py:206
  133.4 1.0 shard_map.56
  (28 shorter events, 0.2 us)
Async XLA Ops:
  6.5 1.1 copy-start
  6.5 2.6 %copy-start.2 = (s32[1,1,2]{2,1,0:T(1,128)S(1)}, s32[1,1,2]{2,1,0:T(1,128)}, u32[]{:S(2)}) copy-start(s32[1,1,2]{2,1,0:T(1,128)} %param.6) | copy-start | bytes 28
  6.5 94.3 %all-gather.3.cloned.1.call-start = ((), (), s32[]{:S(2)}) async-start(), calls=%async_computation.1 | async-start | bytes 12976128 | tf_op jit(solution)/shard_map/all_gather | solution.py:151
  11.5 14.7 %collective-permute-start = (bf16[272,512]{1,0:T(8,128)(2,1)S(1)}, bf16[272,512]{1,0:T(8,128)(2,1)S(1)}, u32[]{:S(2)}, u32[]{:S(2)}) collective-permute-start(bf16[272,512]{1,0:T(8,128)(2,1)S(1)} %concatenate.40), channel_id=1, source_target_pairs={{0,2},{1,7},{2,4},{3,1},{4,6},{5,3},{6,0},{7,5},{8,10},{9,15},{10,... | collective-permute-start | bytes 835592 | tf_op jit(solution)/shard_map/ppermute | solution.py:29
  15.3 17.7 %collective-permute-start.6 = (bf16[272,512]{1,0:T(8,128)(2,1)S(1)}, bf16[272,512]{1,0:T(8,128)(2,1)S(1)}, u32[]{:S(2)}, u32[]{:S(2)}) collective-permute-start(bf16[272,512]{1,0:T(8,128)(2,1)S(1)} %concatenate.46), channel_id=1, source_target_pairs={{0,8},{1,25},{2,10},{3,27},{4,12},{5,29},{6,14},{7,31},{8,16},{9,1... | collective-permute-start | bytes 835592 | tf_op jit(solution)/shard_map/ppermute | solution.py:29
  18.7 16.3 %collective-permute-start.1 = (bf16[272,512]{1,0:T(8,128)(2,1)S(1)}, bf16[272,512]{1,0:T(8,128)(2,1)S(1)}, u32[]{:S(2)}, u32[]{:S(2)}) collective-permute-start(bf16[272,512]{1,0:T(8,128)(2,1)S(1)} %concatenate.40), channel_id=1, source_target_pairs={{0,6},{1,3},{2,0},{3,5},{4,2},{5,7},{6,4},{7,1},{8,14},{9,11},{10,... | collective-permute-start | bytes 835592 | tf_op jit(solution)/shard_map/ppermute | solution.py:29
  21.4 13.7 %collective-permute-start.7 = (bf16[272,512]{1,0:T(8,128)(2,1)S(1)}, bf16[272,512]{1,0:T(8,128)(2,1)S(1)}, u32[]{:S(2)}, u32[]{:S(2)}) collective-permute-start(bf16[272,512]{1,0:T(8,128)(2,1)S(1)} %concatenate.46), channel_id=1, source_target_pairs={{0,24},{1,9},{2,26},{3,11},{4,28},{5,13},{6,30},{7,15},{8,0},{9,17... | collective-permute-start | bytes 835592 | tf_op jit(solution)/shard_map/ppermute | solution.py:29
  26.2 21.6 %collective-permute-start.2 = (bf16[272,512]{1,0:T(8,128)(2,1)S(1)}, bf16[272,512]{1,0:T(8,128)(2,1)S(1)}, u32[]{:S(2)}, u32[]{:S(2)}) collective-permute-start(bf16[272,512]{1,0:T(8,128)(2,1)S(1)} %collective-permute-done), channel_id=1, source_target_pairs={{0,2},{1,7},{2,4},{3,1},{4,6},{5,3},{6,0},{7,5},{8,10},{9,15},{10,... | collective-permute-start | bytes 835592 | tf_op jit(solution)/shard_map/ppermute | solution.py:29
  33.0 9.7 %collective-permute-start.8 = (bf16[272,512]{1,0:T(8,128)(2,1)S(1)}, bf16[272,512]{1,0:T(8,128)(2,1)S(1)}, u32[]{:S(2)}, u32[]{:S(2)}) collective-permute-start(bf16[272,512]{1,0:T(8,128)(2,1)S(1)} %collective-permute-done.6), channel_id=1, source_target_pairs={{0,8},{1,25},{2,10},{3,27},{4,12},{5,29},{6,14},{7,31},{8,16},{9,1... | collective-permute-start | bytes 835592 | tf_op jit(solution)/shard_map/ppermute | solution.py:29
  35.0 43.1 %copy-start.1 = (s32[4]{0:T(128)S(1)}, s32[4]{0:T(128)}, u32[]{:S(2)}) copy-start(s32[4]{0:T(128)} %constant.81.clone) | copy-start | bytes 52
  42.7 28.1 %collective-permute-start.9 = (bf16[1088,512]{1,0:T(8,128)(2,1)S(1)}, bf16[1088,512]{1,0:T(8,128)(2,1)}, u32[]{:S(2)}, u32[]{:S(2)}) collective-permute-start(bf16[1088,512]{1,0:T(8,128)(2,1)S(1)} %constant_dynamic-update-slice_fusion.5.refs_4_), channel_id=1, source_target_pairs={{0,2},{1,7},{2,4},{3,1},{4,6},{5,3},{6,0},{7,5},{8,10},{9,15},{10,... | collective-permute-start | bytes 3342344 | tf_op jit(solution)/shard_map/ppermute | solution.py:29
  47.9 28.1 %collective-permute-start.3 = (bf16[1088,512]{1,0:T(8,128)(2,1)S(1)}, bf16[1088,512]{1,0:T(8,128)(2,1)}, u32[]{:S(2)}, u32[]{:S(2)}) collective-permute-start(bf16[1088,512]{1,0:T(8,128)(2,1)S(1)} %constant_dynamic-update-slice_fusion.refs_0_), channel_id=1, source_target_pairs={{0,8},{1,25},{2,10},{3,27},{4,12},{5,29},{6,14},{7,31},{8,16},{9,1... | collective-permute-start | bytes 3342344 | tf_op jit(solution)/shard_map/ppermute | solution.py:29
  49.8 28.7 %collective-permute-start.10 = (bf16[1088,512]{1,0:T(8,128)(2,1)S(1)}, bf16[1088,512]{1,0:T(8,128)(2,1)}, u32[]{:S(2)}, u32[]{:S(2)}) collective-permute-start(bf16[1088,512]{1,0:T(8,128)(2,1)S(1)} %constant_dynamic-update-slice_fusion.5.refs_4_), channel_id=1, source_target_pairs={{0,6},{1,3},{2,0},{3,5},{4,2},{5,7},{6,4},{7,1},{8,14},{9,11},{10,... | collective-permute-start | bytes 3342344 | tf_op jit(solution)/shard_map/ppermute | solution.py:29
  51.7 28.4 %collective-permute-start.4 = (bf16[1088,512]{1,0:T(8,128)(2,1)S(1)}, bf16[1088,512]{1,0:T(8,128)(2,1)}, u32[]{:S(2)}, u32[]{:S(2)}) collective-permute-start(bf16[1088,512]{1,0:T(8,128)(2,1)S(1)} %constant_dynamic-update-slice_fusion.refs_0_), channel_id=1, source_target_pairs={{0,24},{1,9},{2,26},{3,11},{4,28},{5,13},{6,30},{7,15},{8,0},{9,17... | collective-permute-start | bytes 3342344 | tf_op jit(solution)/shard_map/ppermute | solution.py:29
  70.7 17.7 %collective-permute-start.11 = (bf16[1088,512]{1,0:T(8,128)(2,1)}, bf16[1088,512]{1,0:T(8,128)(2,1)}, u32[]{:S(2)}, u32[]{:S(2)}) collective-permute-start(bf16[1088,512]{1,0:T(8,128)(2,1)} %collective-permute-done.9.refs_5_), channel_id=1, source_target_pairs={{0,2},{1,7},{2,4},{3,1},{4,6},{5,3},{6,0},{7,5},{8,10},{9,15},{10,... | collective-permute-start | bytes 3342344 | tf_op jit(solution)/shard_map/ppermute | solution.py:29
  76.0 18.9 %collective-permute-start.5 = (bf16[1088,512]{1,0:T(8,128)(2,1)}, bf16[1088,512]{1,0:T(8,128)(2,1)}, u32[]{:S(2)}, u32[]{:S(2)}) collective-permute-start(bf16[1088,512]{1,0:T(8,128)(2,1)} %collective-permute-done.3.refs_1_), channel_id=1, source_target_pairs={{0,8},{1,25},{2,10},{3,27},{4,12},{5,29},{6,14},{7,31},{8,16},{9,1... | collective-permute-start | bytes 3342344 | tf_op jit(solution)/shard_map/ppermute | solution.py:29
  109.3 24.1 %collective-permute-start.12 = (f32[256,384]{1,0:T(8,128)}, f32[256,384]{1,0:T(8,128)S(1)}, u32[]{:S(2)}, u32[]{:S(2)}) collective-permute-start(f32[256,384]{1,0:T(8,128)} %get-tuple-element.10), channel_id=1, source_target_pairs={{0,1},{1,0},{2,3},{3,2},{4,5},{5,4},{6,7},{7,6},{8,9},{9,8},{10,11... | collective-permute-start | bytes 1179656 | tf_op jit(solution)/shard_map/ppermute | solution.py:207
Sparse Core Ops, SparseCore 0:
  9.5 91.3 all-gather.2
